TPU v7x, 1024 devices: a whole 4x8x16 slice. The times are simulated.
1024 devices in a mesh: gx: 32 (over y, z_lo), gz: 32 (over x, z_hi, core).
Axes of the slice: x: 4, y: 8, z: 16 (z_hi: 4, z_lo: 4; z = z_hi * 4 + z_lo), core: 2. Of those that a mesh axis runs over, the one named last changes fastest.
Arguments:
- populations: float32 [19, 128, 512, 128], P(None, 'gx', 'gz'), may hold values from 0.019 to 0.44, as said below
- fluid_mask: int32 [128, 512, 128], P('gx', 'gz'), may hold values 0 or 1
Outputs:
- spectrum: float32 [2, 128, 128, 512], P(None, 'gx', 'gz')
Inputs may be any that keep to these rules, and one draw needn't show every extreme that they name: `populations`: each entry lies between 0.7 and 1.3 times the weight of its velocity.
All inputs are finite; a program needn't handle non-finite values. No bound on the sum of `fluid_mask` on one device may be relied on, other than what follows from the above.
Results may differ from a plain program's by a relative error of at most 0.0003.
Values sent between devices are 32-bit elements; how exact they have to be, the bound alone decides.
No kernel may reach another device: no remote copies, remote signals or barrier semaphores. Data moves between devices by JAX's collectives and lax.ppermute only.
A program may use at most 32 MiB of HBM per device.

v0:
```python
import math

import jax
import jax.numpy as jnp
from jax import lax
from jax.sharding import PartitionSpec as P

VELOCITIES = (
    (0, 0, 0),
    (1, 0, 0),
    (-1, 0, 0),
    (0, 1, 0),
    (0, -1, 0),
    (0, 0, 1),
    (0, 0, -1),
    (1, 1, 0),
    (-1, -1, 0),
    (1, -1, 0),
    (-1, 1, 0),
    (1, 0, 1),
    (-1, 0, -1),
    (1, 0, -1),
    (-1, 0, 1),
    (0, 1, 1),
    (0, -1, -1),
    (0, 1, -1),
    (0, -1, 1),
)
LATTICE_WEIGHTS = (1.0 / 3.0,) + (1.0 / 18.0,) * 6 + (1.0 / 36.0,) * 12
OPPOSITES = (0, 2, 1, 4, 3, 6, 5, 8, 7, 10, 9, 12, 11, 14, 13, 16, 15, 18, 17)
RELAX_TIME = 0.6
BODY_FORCE = 0.0001
SPEED_UNIT = 0.05


def with_halo(cells, sides, width):
    for axis, dim in sides:
        count = lax.axis_size(axis)
        head = lax.slice_in_dim(cells, 0, width, axis=dim)
        tail = lax.slice_in_dim(cells, cells.shape[dim] - width, cells.shape[dim], axis=dim)
        cells = jnp.concatenate(
            [
                lax.ppermute(tail, axis, [(i, (i + 1) % count) for i in range(count)]),
                cells,
                lax.ppermute(head, axis, [((i + 1) % count, i) for i in range(count)]),
            ],
            axis=dim,
        )
    return cells


def component(which, float_type):
    return jnp.asarray([velocity[which] for velocity in VELOCITIES], float_type).reshape(
        19, 1, 1, 1
    )


def collide(current, fluid_cells):
    float_type = current.dtype
    along_x = component(0, float_type)
    along_y = component(1, float_type)
    along_z = component(2, float_type)
    weights = jnp.asarray(LATTICE_WEIGHTS, float_type).reshape(19, 1, 1, 1)
    density = jnp.sum(current, axis=0)
    speed_x = jnp.sum(along_x * current, axis=0) / density
    speed_y = jnp.sum(along_y * current, axis=0) / density
    speed_z = jnp.sum(along_z * current, axis=0) / density
    project = along_x * speed_x + along_y * speed_y + along_z * speed_z
    square = speed_x * speed_x + speed_y * speed_y + speed_z * speed_z
    balance = weights * density * (1.0 + 3.0 * project + 4.5 * project * project - 1.5 * square)
    relaxed = (
        current - (current - balance) / RELAX_TIME + 3.0 * BODY_FORCE * weights * along_x * density
    )
    return jnp.where(fluid_cells > 0, relaxed, current)


def stream(padded):
    extent_x = padded.shape[1] - 2
    extent_z = padded.shape[2] - 2
    height = padded.shape[3]
    walled = jnp.pad(padded, ((0, 0), (0, 0), (0, 0), (1, 1)))
    fluid_self = padded[19, 1 : 1 + extent_x, 1 : 1 + extent_z, :]
    results = []
    for number in range(19):
        step_x, step_y, step_z = VELOCITIES[number]
        start_x = 1 - step_x
        start_z = 1 - step_z
        start_y = 1 - step_y
        source_value = walled[
            number,
            start_x : start_x + extent_x,
            start_z : start_z + extent_z,
            start_y : start_y + height,
        ]
        source_fluid = walled[
            19,
            start_x : start_x + extent_x,
            start_z : start_z + extent_z,
            start_y : start_y + height,
        ]
        bounce = padded[OPPOSITES[number], 1 : 1 + extent_x, 1 : 1 + extent_z, :]
        own_value = padded[number, 1 : 1 + extent_x, 1 : 1 + extent_z, :]
        arrived = jnp.where(source_fluid > 0, source_value, bounce)
        results.append(jnp.where(fluid_self > 0, arrived, own_value))
    return jnp.stack(results, axis=0)


def dft_tables(length, factor):
    index = jnp.arange(length, dtype=jnp.int32)
    products = index[:, None] * index[None, :] % length
    angles = products.astype(jnp.float32) * (2.0 * math.pi / length)
    return (jnp.cos(angles) * factor, jnp.sin(angles) * factor)


def shards(populations, fluid_mask):
    fluid_cells = fluid_mask.astype(jnp.float32)
    current = populations
    for repeat in range(2):
        relaxed = collide(current, fluid_cells)
        stacked = jnp.concatenate([relaxed, fluid_cells[None]], axis=0)
        padded = with_halo(stacked, (("gx", 1), ("gz", 2)), 1)
        current = stream(padded)
    along_x = component(0, jnp.float32)
    density = jnp.sum(current, axis=0)
    speed_x = fluid_cells * jnp.sum(along_x * current, axis=0) / density
    columns = jnp.transpose(speed_x, (2, 1, 0))
    full_x = speed_x.shape[0] * lax.axis_size("gx")
    full_z = speed_x.shape[1] * lax.axis_size("gz")
    norm_scale = 1.0 / (math.sqrt(full_x * full_z) * SPEED_UNIT)
    highest = lax.Precision.HIGHEST
    block = lax.all_to_all(columns, "gx", split_axis=0, concat_axis=2, tiled=True)
    cosine, sine = dft_tables(block.shape[2], norm_scale)
    real_part = jnp.einsum("yzx,xk->yzk", block, cosine, precision=highest)
    imag_part = -jnp.einsum("yzx,xk->yzk", block, sine, precision=highest)
    along_kx = jnp.stack([real_part, imag_part], axis=0)
    block = lax.all_to_all(along_kx, "gz", split_axis=3, concat_axis=2, tiled=True)
    cosine, sine = dft_tables(block.shape[2], 1.0)
    real_in = block[0]
    imag_in = block[1]
    real_part = jnp.einsum("ync,nk->yck", real_in, cosine, precision=highest) + jnp.einsum(
        "ync,nk->yck", imag_in, sine, precision=highest
    )
    imag_part = jnp.einsum("ync,nk->yck", imag_in, cosine, precision=highest) - jnp.einsum(
        "ync,nk->yck", real_in, sine, precision=highest
    )
    return jnp.stack([real_part, imag_part], axis=0)


def solution(mesh):
    placed = (P(None, "gx", "gz", None), P("gx", "gz", None))
    return jax.shard_map(
        shards, mesh=mesh, in_specs=placed, out_specs=P(None, "gx", "gz", None), check_vma=False
    )
```

profile of v0, /device:TPU:1, one launch (start us, length us, event | category | flops | bytes accessed | tf_op | source)
XLA Modules:
  0.0 147.4 jit_solution(6747621221019265592)
XLA Ops:
  0.0 0.8 convert_compare_fusion
  0.8 0.8 convert_bitcast_fusion
  1.6 1.3 multiply_reduce_fusion.6
  3.0 1.2 fusion.50
  4.2 11.4 %collective-permute-start.1 = (f32[20,1,16,128]{3,2,1,0:T(8,128)S(1)}, f32[20,1,16,128]{3,2,1,0:T(8,128)S(1)}, u32[]{:S(2)}, u32[]{:S(2)}) collective-permute-start(f32[20,1,16,128]{3,2,1,0:T(8,128)S(1)} %get-tuple-element.64), channel_id=1, source_target_pairs={{32,0},{64,32},{96,64},{128,96},{160,128},{192,160},{224,192},{256... | collective-permute-start | bytes 491528 | tf_op jit(solution)/shard_map/ppermute | solution.py:45
  15.6 1.9 %collective-permute-start = (f32[20,1,16,128]{3,2,1,0:T(8,128)S(1)}, f32[20,1,16,128]{3,2,1,0:T(8,128)S(1)}, u32[]{:S(2)}, u32[]{:S(2)}) collective-permute-start(f32[20,1,16,128]{3,2,1,0:T(8,128)S(1)} %get-tuple-element.65), channel_id=1, source_target_pairs={{0,32},{32,64},{64,96},{96,128},{128,160},{160,192},{192,224},{224... | collective-permute-start | bytes 491528 | tf_op jit(solution)/shard_map/ppermute | solution.py:43
  17.8 7.7 %collective-permute-done = f32[20,1,16,128]{3,2,1,0:T(8,128)S(1)} collective-permute-done((f32[20,1,16,128]{3,2,1,0:T(8,128)S(1)}, f32[20,1,16,128]{3,2,1,0:T(8,128)S(1)}, u32[]{:S(2)}, u32[]{:S(2)}) %collective-permute-start) | collective-permute-done | bytes 163872 | tf_op jit(solution)/shard_map/ppermute | solution.py:43
  25.7 7.8 %collective-permute-start.3 = (f32[20,6,1,128]{3,2,1,0:T(1,128)S(1)}, f32[20,6,1,128]{3,2,1,0:T(1,128)S(1)}, u32[]{:S(2)}, u32[]{:S(2)}) collective-permute-start(f32[20,6,1,128]{3,2,1,0:T(1,128)S(1)} %get-tuple-element.57), channel_id=1, source_target_pairs={{1,0},{2,1},{3,2},{4,3},{5,4},{6,5},{7,6},{8,7},{9,8},{10,9},{11,1... | collective-permute-start | bytes 184328 | tf_op jit(solution)/shard_map/ppermute | solution.py:45
  33.5 7.1 %collective-permute-start.2 = (f32[20,6,1,128]{3,2,1,0:T(1,128)S(1)}, f32[20,6,1,128]{3,2,1,0:T(1,128)S(1)}, u32[]{:S(2)}, u32[]{:S(2)}) collective-permute-start(f32[20,6,1,128]{3,2,1,0:T(1,128)S(1)} %get-tuple-element.56), channel_id=1, source_target_pairs={{0,1},{1,2},{2,3},{3,4},{4,5},{5,6},{6,7},{7,8},{8,9},{9,10},{10,1... | collective-permute-start | bytes 184328 | tf_op jit(solution)/shard_map/ppermute | solution.py:43
  40.8 5.9 %collective-permute-done.2 = f32[20,6,1,128]{3,2,1,0:T(1,128)S(1)} collective-permute-done((f32[20,6,1,128]{3,2,1,0:T(1,128)S(1)}, f32[20,6,1,128]{3,2,1,0:T(1,128)S(1)}, u32[]{:S(2)}, u32[]{:S(2)}) %collective-permute-start.2) | collective-permute-done | bytes 61472 | tf_op jit(solution)/shard_map/ppermute | solution.py:43
  48.4 0.4 copy-done.2
  49.5 0.5 fusion.58
  50.0 2.7 %collective-permute-start.5 = (f32[20,1,16,128]{3,2,1,0:T(8,128)S(1)}, f32[20,1,16,128]{3,2,1,0:T(8,128)S(1)}, u32[]{:S(2)}, u32[]{:S(2)}) collective-permute-start(f32[20,1,16,128]{3,2,1,0:T(8,128)S(1)} %get-tuple-element.60), channel_id=1, source_target_pairs={{32,0},{64,32},{96,64},{128,96},{160,128},{192,160},{224,192},{256... | collective-permute-start | bytes 491528 | tf_op jit(solution)/shard_map/ppermute | solution.py:45
  52.7 2.6 %collective-permute-start.4 = (f32[20,1,16,128]{3,2,1,0:T(8,128)S(1)}, f32[20,1,16,128]{3,2,1,0:T(8,128)S(1)}, u32[]{:S(2)}, u32[]{:S(2)}) collective-permute-start(f32[20,1,16,128]{3,2,1,0:T(8,128)S(1)} %get-tuple-element.61), channel_id=1, source_target_pairs={{0,32},{32,64},{64,96},{96,128},{128,160},{160,192},{192,224},{224... | collective-permute-start | bytes 491528 | tf_op jit(solution)/shard_map/ppermute | solution.py:43
  55.3 2.5 %collective-permute-done.5 = f32[20,1,16,128]{3,2,1,0:T(8,128)S(1)} collective-permute-done((f32[20,1,16,128]{3,2,1,0:T(8,128)S(1)}, f32[20,1,16,128]{3,2,1,0:T(8,128)S(1)}, u32[]{:S(2)}, u32[]{:S(2)}) %collective-permute-start.5) | collective-permute-done | bytes 163872 | tf_op jit(solution)/shard_map/ppermute | solution.py:45
  57.9 4.8 %collective-permute-done.4 = f32[20,1,16,128]{3,2,1,0:T(8,128)S(1)} collective-permute-done((f32[20,1,16,128]{3,2,1,0:T(8,128)S(1)}, f32[20,1,16,128]{3,2,1,0:T(8,128)S(1)}, u32[]{:S(2)}, u32[]{:S(2)}) %collective-permute-start.4) | collective-permute-done | bytes 163872 | tf_op jit(solution)/shard_map/ppermute | solution.py:43
  62.8 14.3 %collective-permute-start.7 = (f32[20,6,1,128]{3,2,1,0:T(1,128)S(1)}, f32[20,6,1,128]{3,2,1,0:T(1,128)S(1)}, u32[]{:S(2)}, u32[]{:S(2)}) collective-permute-start(f32[20,6,1,128]{3,2,1,0:T(1,128)S(1)} %get-tuple-element.53), channel_id=1, source_target_pairs={{1,0},{2,1},{3,2},{4,3},{5,4},{6,5},{7,6},{8,7},{9,8},{10,9},{11,1... | collective-permute-start | bytes 184328 | tf_op jit(solution)/shard_map/ppermute | solution.py:45
  77.2 1.9 %collective-permute-start.6 = (f32[20,6,1,128]{3,2,1,0:T(1,128)S(1)}, f32[20,6,1,128]{3,2,1,0:T(1,128)S(1)}, u32[]{:S(2)}, u32[]{:S(2)}) collective-permute-start(f32[20,6,1,128]{3,2,1,0:T(1,128)S(1)} %get-tuple-element.52), channel_id=1, source_target_pairs={{0,1},{1,2},{2,3},{3,4},{4,5},{5,6},{6,7},{7,8},{8,9},{9,10},{10,1... | collective-permute-start | bytes 184328 | tf_op jit(solution)/shard_map/ppermute | solution.py:43
  79.3 1.1 collective-permute-done.6
  82.7 12.9 %all_to_all.33 = f32[32,1,256]{2,1,0:T(1,128)S(1)} all-to-all(f32[32,1,256]{2,1,0:T(1,128)S(1)} %reshape.315), channel_id=1, replica_groups=mesh['gx'=32,'gz'=32] {'gx'}, dimensions={0} | all-to-all | bytes 65536 | tf_op jit(solution)/shard_map/all_to_all | solution.py:131
  95.6 0.5 broadcast.366
  96.1 0.7 reduce.38
  97.3 0.7 fusion.22
  97.9 0.6 convolution_bitcast_fusion
  98.9 0.4 reshape.317
  99.3 27.1 %all_to_all.34 = f32[32,1,512]{2,1,0:T(1,128)S(1)} all-to-all(f32[32,1,512]{2,1,0:T(1,128)S(1)} %reshape.317), channel_id=1, replica_groups=mesh['gx'=32,'gz'=32] {'gz'}, dimensions={0} | all-to-all | bytes 131072 | tf_op jit(solution)/shard_map/all_to_all | solution.py:136
  126.4 0.8 reduce.39
  127.9 4.6 %fusion.28 = f32[4,4,512]{2,1,0:T(4,128)S(1)} fusion(f32[4,512,4]{1,2,0:T(4,128)S(1)} %squeeze.378), kind=kOutput, calls=%fused_computation.87 | convolution fusion | flops 54001664 | bytes 65536 | tf_op jit(solution)/shard_map/ync,nk->yck/dot_general | solution.py:143
  132.7 4.6 %fusion.30 = f32[4,4,512]{2,1,0:T(4,128)S(1)} fusion(f32[4,512,4]{1,2,0:T(4,128)S(1)} %squeeze.377), kind=kOutput, calls=%fused_computation.89 | convolution fusion | flops 54001664 | bytes 65536 | tf_op jit(solution)/shard_map/ync,nk->yck/dot_general | solution.py:140
  137.4 4.7 %fusion.20 = f32[1,4,4,512]{3,2,1,0:T(4,128)S(1)} fusion(f32[4,4,512]{2,1,0:T(4,128)S(1)} %fusion.28, f32[4,512,4]{1,2,0:T(4,128)S(1)} %squeeze.377), kind=kOutput, calls=%fused_computation.76 | convolution fusion | flops 54009856 | bytes 98304 | tf_op jit(solution)/shard_map/ync,nk->yck/dot_general | solution.py:143
  142.1 4.7 %fusion.21 = f32[1,4,4,512]{3,2,1,0:T(4,128)S(1)} fusion(f32[4,4,512]{2,1,0:T(4,128)S(1)} %fusion.30, f32[4,512,4]{1,2,0:T(4,128)S(1)} %squeeze.378), kind=kOutput, calls=%fused_computation.78 | convolution fusion | flops 54009856 | bytes 98304 | tf_op jit(solution)/shard_map/ync,nk->yck/dot_general | solution.py:140
  146.7 0.6 pad_maximum_fusion.15
  (86 shorter events, 6.8 us)
Async XLA Ops:
  0.0 2.9 %copy-start.1 = (f32[19,4,16,128]{3,2,1,0:T(8,128)S(1)}, f32[19,4,16,128]{3,2,1,0:T(8,128)}, u32[]{:S(2)}) copy-start(f32[19,4,16,128]{3,2,1,0:T(8,128)} %param.11) | copy-start | bytes 1867780
  4.2 13.6 %collective-permute-start.1 = (f32[20,1,16,128]{3,2,1,0:T(8,128)S(1)}, f32[20,1,16,128]{3,2,1,0:T(8,128)S(1)}, u32[]{:S(2)}, u32[]{:S(2)}) collective-permute-start(f32[20,1,16,128]{3,2,1,0:T(8,128)S(1)} %get-tuple-element.64), channel_id=1, source_target_pairs={{32,0},{64,32},{96,64},{128,96},{160,128},{192,160},{224,192},{256... | collective-permute-start | bytes 491528 | tf_op jit(solution)/shard_map/ppermute | solution.py:45
  15.6 10.0 %collective-permute-start = (f32[20,1,16,128]{3,2,1,0:T(8,128)S(1)}, f32[20,1,16,128]{3,2,1,0:T(8,128)S(1)}, u32[]{:S(2)}, u32[]{:S(2)}) collective-permute-start(f32[20,1,16,128]{3,2,1,0:T(8,128)S(1)} %get-tuple-element.65), channel_id=1, source_target_pairs={{0,32},{32,64},{64,96},{96,128},{128,160},{160,192},{192,224},{224... | collective-permute-start | bytes 491528 | tf_op jit(solution)/shard_map/ppermute | solution.py:43
  25.6 15.1 %copy-start = (s32[4,16,128]{2,1,0:T(8,128)S(1)}, s32[4,16,128]{2,1,0:T(8,128)}, u32[]{:S(2)}) copy-start(s32[4,16,128]{2,1,0:T(8,128)} %param.12) | copy-start | bytes 98308
  25.7 15.1 %collective-permute-start.3 = (f32[20,6,1,128]{3,2,1,0:T(1,128)S(1)}, f32[20,6,1,128]{3,2,1,0:T(1,128)S(1)}, u32[]{:S(2)}, u32[]{:S(2)}) collective-permute-start(f32[20,6,1,128]{3,2,1,0:T(1,128)S(1)} %get-tuple-element.57), channel_id=1, source_target_pairs={{1,0},{2,1},{3,2},{4,3},{5,4},{6,5},{7,6},{8,7},{9,8},{10,9},{11,1... | collective-permute-start | bytes 184328 | tf_op jit(solution)/shard_map/ppermute | solution.py:45
  33.5 13.2 %collective-permute-start.2 = (f32[20,6,1,128]{3,2,1,0:T(1,128)S(1)}, f32[20,6,1,128]{3,2,1,0:T(1,128)S(1)}, u32[]{:S(2)}, u32[]{:S(2)}) collective-permute-start(f32[20,6,1,128]{3,2,1,0:T(1,128)S(1)} %get-tuple-element.56), channel_id=1, source_target_pairs={{0,1},{1,2},{2,3},{3,4},{4,5},{5,6},{6,7},{7,8},{8,9},{9,10},{10,1... | collective-permute-start | bytes 184328 | tf_op jit(solution)/shard_map/ppermute | solution.py:43
  48.1 0.7 copy-start.2
  48.1 0.7 copy-start.3
  48.2 0.7 copy-start.4
  48.8 0.7 copy-start.5
  48.8 0.7 copy-start.6
  50.0 7.8 %collective-permute-start.5 = (f32[20,1,16,128]{3,2,1,0:T(8,128)S(1)}, f32[20,1,16,128]{3,2,1,0:T(8,128)S(1)}, u32[]{:S(2)}, u32[]{:S(2)}) collective-permute-start(f32[20,1,16,128]{3,2,1,0:T(8,128)S(1)} %get-tuple-element.60), channel_id=1, source_target_pairs={{32,0},{64,32},{96,64},{128,96},{160,128},{192,160},{224,192},{256... | collective-permute-start | bytes 491528 | tf_op jit(solution)/shard_map/ppermute | solution.py:45
  52.7 10.0 %collective-permute-start.4 = (f32[20,1,16,128]{3,2,1,0:T(8,128)S(1)}, f32[20,1,16,128]{3,2,1,0:T(8,128)S(1)}, u32[]{:S(2)}, u32[]{:S(2)}) collective-permute-start(f32[20,1,16,128]{3,2,1,0:T(8,128)S(1)} %get-tuple-element.61), channel_id=1, source_target_pairs={{0,32},{32,64},{64,96},{96,128},{128,160},{160,192},{192,224},{224... | collective-permute-start | bytes 491528 | tf_op jit(solution)/shard_map/ppermute | solution.py:43
  62.8 16.4 %collective-permute-start.7 = (f32[20,6,1,128]{3,2,1,0:T(1,128)S(1)}, f32[20,6,1,128]{3,2,1,0:T(1,128)S(1)}, u32[]{:S(2)}, u32[]{:S(2)}) collective-permute-start(f32[20,6,1,128]{3,2,1,0:T(1,128)S(1)} %get-tuple-element.53), channel_id=1, source_target_pairs={{1,0},{2,1},{3,2},{4,3},{5,4},{6,5},{7,6},{8,7},{9,8},{10,9},{11,1... | collective-permute-start | bytes 184328 | tf_op jit(solution)/shard_map/ppermute | solution.py:45
  77.2 3.2 %collective-permute-start.6 = (f32[20,6,1,128]{3,2,1,0:T(1,128)S(1)}, f32[20,6,1,128]{3,2,1,0:T(1,128)S(1)}, u32[]{:S(2)}, u32[]{:S(2)}) collective-permute-start(f32[20,6,1,128]{3,2,1,0:T(1,128)S(1)} %get-tuple-element.52), channel_id=1, source_target_pairs={{0,1},{1,2},{2,3},{3,4},{4,5},{5,6},{6,7},{7,8},{8,9},{9,10},{10,1... | collective-permute-start | bytes 184328 | tf_op jit(solution)/shard_map/ppermute | solution.py:43
where the time goes:
time: 148 us; the launch traced here: 147 us
  starting transfers between devices  49.7 us (34%)
  blocking collectives  40 us (27%)
  waiting for transfers between devices  22.4 us (15%)
  matrix products  19.9 us (13%)
  other arithmetic  11 us (7%)
  local copies, waits for them, and re-layouts  3.71 us (3%)
    ppermute x4, starting transfers between devices, with_halo(): lax.ppermute(head, axis, [((i + 1) % count, i) for i in range(count)])  36.1 us
    all_to_all x1, blocking collectives, shards(): lax.all_to_all(along_kx, 'gz', split_axis=3, concat_axis=2, tiled=True)  27.1 us
    ppermute x4, waiting for transfers between devices, with_halo(): lax.ppermute(tail, axis, [(i, (i + 1) % count) for i in range(count)])  19.6 us
    ppermute x4, starting transfers between devices, with_halo(): lax.ppermute(tail, axis, [(i, (i + 1) % count) for i in range(count)])  13.6 us
    all_to_all x1, blocking collectives, shards(): lax.all_to_all(columns, 'gx', split_axis=0, concat_axis=2, tiled=True)  12.9 us
    dot_general x1, matrix products, shards(): jnp.einsum('ync,nk->yck', real_in, sine, precision=highest)  4.67 us
    dot_general x1, matrix products, shards(): jnp.einsum('ync,nk->yck', imag_in, sine, precision=highest)  4.67 us
    dot_general x1, matrix products, shards(): jnp.einsum('ync,nk->yck', real_in, cosine, precision=highest)  4.63 us
  transfers between devices with their start and end apart: 8, of which 6 were waited for; matrix products, arithmetic and copies ran while one was open for 0% of the time, Pallas kernels for 0%

commit v1 on v0

v1 whole, which is shorter than its diff:
```python
import math

import jax
import jax.numpy as jnp
import ml_dtypes
import numpy as np
from jax import lax
from jax.experimental import pallas as pl
from jax.experimental.pallas import tpu as pltpu
from jax.sharding import PartitionSpec as P

VELOCITIES = (
    (0, 0, 0),
    (1, 0, 0),
    (-1, 0, 0),
    (0, 1, 0),
    (0, -1, 0),
    (0, 0, 1),
    (0, 0, -1),
    (1, 1, 0),
    (-1, -1, 0),
    (1, -1, 0),
    (-1, 1, 0),
    (1, 0, 1),
    (-1, 0, -1),
    (1, 0, -1),
    (-1, 0, 1),
    (0, 1, 1),
    (0, -1, -1),
    (0, 1, -1),
    (0, -1, 1),
)
WEIGHTS = (1.0 / 3.0,) + (1.0 / 18.0,) * 6 + (1.0 / 36.0,) * 12
OPPOSITES = (0, 2, 1, 4, 3, 6, 5, 8, 7, 10, 9, 12, 11, 14, 13, 16, 15, 18, 17)
OMEGA = 1.0 / 0.6
BODY_FORCE = 0.0001
SPEED_UNIT = 0.05

DEVICES_X = 32
DEVICES_Z = 32
LAYERS = 4
COLUMNS = 16
HEIGHT = 128
NX = 128
NZ = 512
MASK = 19
RING = 24

X_UP = tuple(i for i in range(19) if VELOCITIES[i][0] == 1)
X_DOWN = tuple(i for i in range(19) if VELOCITIES[i][0] == -1)
Z_UP = tuple(i for i in range(19) if VELOCITIES[i][2] == 1)
Z_DOWN = tuple(i for i in range(19) if VELOCITIES[i][2] == -1)
Z_UNITS_UP = tuple((i, 0) for i in range(20)) + tuple((i, 1) for i in Z_UP + (MASK,))
Z_UNITS_DOWN = tuple((i, 0) for i in range(20)) + tuple((i, 1) for i in Z_DOWN + (MASK,))
Z_ROWS = len(Z_UNITS_UP) * LAYERS
X_ROWS = 6 * RING

PARAMS = pltpu.CompilerParams(vmem_limit_bytes=32 * 1024 * 1024)


def relax(current, fluid):
    plus = lambda ids: sum(current[i] for i in ids[1:]) + current[ids[0]]
    right, left = plus(X_UP), plus(X_DOWN)
    rho = plus(tuple(i for i in range(19) if VELOCITIES[i][0] == 0)) + right + left
    flow_x = right - left
    flow_y = plus(tuple(i for i in range(19) if VELOCITIES[i][1] == 1)) - plus(
        tuple(i for i in range(19) if VELOCITIES[i][1] == -1)
    )
    flow_z = plus(Z_UP) - plus(Z_DOWN)
    inverse = 1.0 / rho
    ux, uy, uz = flow_x * inverse, flow_y * inverse, flow_z * inverse
    scaled = rho * OMEGA
    rest = scaled * (1.0 - 1.5 * (ux * ux + uy * uy + uz * uz))
    odd_scale = 3.0 * scaled
    even_scale = 4.5 * scaled
    push = (3.0 * BODY_FORCE) * rho
    out = [None] * 19
    keep = 1.0 - OMEGA
    out[0] = jnp.where(fluid, keep * current[0] + WEIGHTS[0] * rest, current[0])
    for i in range(1, 19, 2):
        cx, cy, cz = VELOCITIES[i]
        parts = [u if c == 1 else -u for c, u in ((cx, ux), (cy, uy), (cz, uz)) if c]
        along = parts[0] if len(parts) == 1 else parts[0] + parts[1]
        even = WEIGHTS[i] * (rest + even_scale * (along * along))
        odd = odd_scale * along
        if cx:
            odd = odd + push if cx == 1 else odd - push
        odd = WEIGHTS[i] * odd
        j = OPPOSITES[i]
        out[i] = jnp.where(fluid, keep * current[i] + (even + odd), current[i])
        out[j] = jnp.where(fluid, keep * current[j] + (even - odd), current[j])
    return out


def collide_kernel(pop, mask, relaxed, up, down):
    for x in range(LAYERS):
        fluid_here = mask[x].astype(jnp.float32)
        out = relax([pop[i, x] for i in range(19)], fluid_here > 0)
        for i in range(19):
            relaxed[i, x] = out[i]
        for send, units, edge, step in (
            (up, Z_UNITS_UP, COLUMNS - 1, -1),
            (down, Z_UNITS_DOWN, 0, 1),
        ):
            for u, (i, depth) in enumerate(units):
                z = edge + step * depth
                value = fluid_here if i == MASK else out[i]
                send[u * LAYERS + x : u * LAYERS + x + 1, :] = value[z : z + 1, :]


def ring_tile(i, x, below, above, row):
    one = lambda ref, u: jnp.broadcast_to(ref[u * LAYERS + x : u * LAYERS + x + 1, :], (8, HEIGHT))
    tile = jnp.where(row < 4, one(above, i), one(below, i))
    if (i, 1) in Z_UNITS_DOWN:
        tile = jnp.where(row == 1, one(above, Z_UNITS_DOWN.index((i, 1))), tile)
    if (i, 1) in Z_UNITS_UP:
        tile = jnp.where(row == 6, one(below, Z_UNITS_UP.index((i, 1))), tile)
    return tile


def face_kernel(relaxed, mask, below, above, right, left):
    row = lax.broadcasted_iota(jnp.int32, (8, HEIGHT), 0)
    for send, ids, x in ((right, X_UP, LAYERS - 1), (left, X_DOWN, 0)):
        for v, i in enumerate(ids + (MASK,)):
            own = mask[x].astype(jnp.float32) if i == MASK else relaxed[i, x]
            send[v * RING : v * RING + COLUMNS, :] = own
            send[v * RING + COLUMNS : (v + 1) * RING, :] = ring_tile(i, x, below, above, row)


def step_kernel(relaxed, mask, below, above, from_left, from_right, out, first, second, planes):
    row = lax.broadcasted_iota(jnp.int32, (8, HEIGHT), 0)
    lane = lax.broadcasted_iota(jnp.int32, (RING, HEIGHT), 1)
    for i in range(20):
        for x in range(LAYERS):
            own = mask[x].astype(jnp.float32) if i == MASK else relaxed[i, x]
            first[i, x, 0:COLUMNS] = own
            first[i, x, COLUMNS:RING] = ring_tile(i, x, below, above, row)

    def moved(value, cy, cz):
        if cz:
            value = pltpu.roll(value, cz % RING, 0)
        if cy:
            value = pltpu.roll(value, cy % HEIGHT, 1)
        return value

    def fluid_moved(value, cy, cz):
        value = moved(value, cy, cz)
        if cy:
            value = jnp.where(lane == (0 if cy == 1 else HEIGHT - 1), 0.0, value)
        return value > 0

    def face(ref, ids, i):
        v = 5 if i == MASK else ids.index(i)
        return ref[v * RING : (v + 1) * RING, :]

    def fluid_at(x):
        if x < 0:
            return face(from_left, X_UP, MASK)
        if x >= LAYERS:
            return face(from_right, X_DOWN, MASK)
        return first[MASK, x]

    def source(i, x):
        if x < 0:
            return face(from_left, X_UP, i)
        if x >= LAYERS:
            return face(from_right, X_DOWN, i)
        return first[i, x]

    for x in range(LAYERS):
        fluid = fluid_at(x) > 0
        arrived = []
        for i in range(19):
            cx, cy, cz = VELOCITIES[i]
            own = first[i, x]
            if i == 0:
                arrived.append(own)
                continue
            open_path = fluid_moved(fluid_at(x - cx), cy, cz)
            value = jnp.where(open_path, moved(source(i, x - cx), cy, cz), first[OPPOSITES[i], x])
            arrived.append(jnp.where(fluid, value, own))
        for i, value in enumerate(relax(arrived, fluid)):
            second[i, x] = value

    zero = jnp.zeros((RING, HEIGHT), jnp.float32)
    for x in range(LAYERS):
        fluid = fluid_at(x) > 0
        groups = {-1: zero, 0: second[0, x], 1: zero}
        for i in range(1, 19):
            cx, cy, cz = VELOCITIES[i]
            open_path = fluid_moved(fluid_at(x - cx), cy, cz)
            inside = 0 <= x - cx < LAYERS
            value = moved(second[i, x - cx], cy, cz) if inside else zero
            groups[cx] = groups[cx] + jnp.where(open_path, value, second[OPPOSITES[i], x])
        number = jnp.where(fluid, groups[1] - groups[-1], 0.0)
        density = jnp.where(fluid, groups[0] + groups[1] + groups[-1], 1.0)
        planes[x * COLUMNS : (x + 1) * COLUMNS, :] = number[0:COLUMNS]
        planes[64 + x * COLUMNS : 64 + (x + 1) * COLUMNS, :] = density[0:COLUMNS]
    transposed = jnp.transpose(planes[...]).reshape(16, 8, HEIGHT)

    for slot, ids, x, target in ((0, X_DOWN, 0, -1), (1, X_UP, LAYERS - 1, LAYERS)):
        total = zero
        for i in ids:
            _, cy, cz = VELOCITIES[i]
            open_path = fluid_moved(fluid_at(x), cy, cz)
            total = total + jnp.where(open_path, moved(second[i, x], cy, cz), 0.0)
        total = jnp.where(fluid_at(target) > 0, total, 0.0)
        planes[slot * COLUMNS : (slot + 1) * COLUMNS, :] = total[0:COLUMNS]
    edges = jnp.transpose(planes[...]).reshape(16, 8, HEIGHT)
    for k in range(16):
        a, b = transposed[k], edges[k]
        out[16 * k : 16 * k + 8, :] = jnp.where(row < 4, a, pltpu.roll(b, 4, 0))
        out[16 * k + 8 : 16 * k + 16, :] = jnp.where(row < 4, pltpu.roll(a, 4, 0), b)


def split(value):
    high = value.astype(jnp.bfloat16)
    return high, (value - high.astype(jnp.float32)).astype(jnp.bfloat16)


def dot(a, b):
    return jnp.dot(a, b, preferred_element_type=jnp.float32)


def product(a, b):
    (a_high, a_low), (b_high, b_low) = a, b
    return dot(a_high, b_high) + (dot(a_high, b_low) + dot(a_low, b_high))


def along_x_kernel(got, high, low, out):
    lane = lax.broadcasted_iota(jnp.int32, (DEVICES_X, HEIGHT), 1)
    speeds = []
    for y in range(4):
        own = got[pl.ds(y, DEVICES_X, stride=8), :]
        edge = got[pl.ds(4 + y, DEVICES_X, stride=8), :]
        from_left = pltpu.roll(edge, 1, 0)
        from_right = pltpu.roll(edge, DEVICES_X - 1, 0)
        total = own + jnp.where(lane < 16, pltpu.roll(from_left, 112, 1), 0.0)
        total = total + jnp.where((lane >= 64) & (lane < 80), pltpu.roll(from_left, 48, 1), 0.0)
        total = total - jnp.where((lane >= 48) & (lane < 64), pltpu.roll(from_right, 48, 1), 0.0)
        total = total + jnp.where(lane >= 112, pltpu.roll(from_right, 112, 1), 0.0)
        density = jnp.where(lane < 64, pltpu.roll(total, 64, 1), 1.0)
        speeds.append(total / density)
    blocks = []
    for shift in (0, 64):
        for x in range(4):
            block = jnp.zeros((DEVICES_X, HEIGHT), jnp.float32)
            for y in range(4):
                start = shift + 16 * y
                piece = pltpu.roll(speeds[y], (start - 16 * x) % HEIGHT, 1)
                block = jnp.where((lane >= start) & (lane < start + 16), piece, block)
            blocks.append(block)
    lines = jnp.concatenate(blocks, axis=0)
    result = product((high[...], low[...]), split(lines))
    for r in range(4):
        out[pl.ds(r, DEVICES_Z, stride=4), :] = result[32 * r : 32 * r + 32, :]


def along_z_kernel(got, one_high, one_low, twist_cos, twist_sin, two_high, two_low, out):
    rows = [got[pl.ds(r, DEVICES_Z, stride=4), :] for r in range(4)]
    lines = jnp.concatenate(
        [
            jnp.concatenate([rows[0], rows[1]], axis=1),
            jnp.concatenate([rows[2], rows[3]], axis=1),
        ],
        axis=0,
    )
    inner = product((one_high[...], one_low[...]), split(lines))
    real, imag = inner[0:32], inner[32:64]
    cosine, sine = twist_cos[...], twist_sin[...]
    turned = jnp.concatenate([real * cosine + imag * sine, imag * cosine - real * sine], axis=0)
    both = product(split(turned), (two_high[...], two_low[...]))
    outer_real = both[0:32, 0:256] + both[32:64, 256:512]
    outer_imag = both[32:64, 0:256] - both[0:32, 256:512]
    for c, value in enumerate((outer_real, outer_imag)):
        columns = jnp.transpose(value)
        wide = columns.reshape(16, 16, 32)
        for quad in range(4):
            parts = [wide[:, 4 * quad + k, :] for k in range(4)]
            tile = jnp.concatenate(parts, axis=1)
            for y in range(4):
                out[c, y, :, 128 * quad : 128 * quad + 128] = tile[4 * y : 4 * y + 4]


def halves(table):
    table = np.asarray(table, np.float32)
    high = table.astype(ml_dtypes.bfloat16)
    low = (table - high.astype(np.float32)).astype(ml_dtypes.bfloat16)
    return high, low


def x_table():
    part, pair, block = np.meshgrid(np.arange(2), np.arange(2), np.arange(32), indexing="ij")
    odd, inner, outer = np.meshgrid(np.arange(2), np.arange(4), np.arange(32), indexing="ij")
    kx = (4 * block + 2 * pair).reshape(-1, 1) + odd.reshape(1, -1)
    x = (4 * outer + inner).reshape(1, -1)
    angle = 2.0 * np.pi * ((kx * x) % NX) / NX
    scale = 1.0 / (math.sqrt(NX * NZ) * SPEED_UNIT)
    return halves(np.where(part.reshape(-1, 1) == 0, np.cos(angle), -np.sin(angle)) * scale)


def z_tables():
    k, b = np.meshgrid(np.arange(32), np.arange(32), indexing="ij")
    angle = 2.0 * np.pi * ((k * b) % 32) / 32
    one = np.block([[np.cos(angle), np.sin(angle)], [-np.sin(angle), np.cos(angle)]])
    angle = 2.0 * np.pi * (np.arange(32)[:, None] * (np.arange(256) % 16)[None, :]) / NZ
    pair, odd, y, z = (v.reshape(-1, 1) for v in np.unravel_index(np.arange(256), (2, 2, 4, 16)))
    y_out, kx_out, k_out = (v.reshape(1, -1) for v in np.unravel_index(np.arange(256), (4, 4, 16)))
    same = (y == y_out) & (2 * pair + odd == kx_out)
    turn = 2.0 * np.pi * ((z * k_out) % 16) / 16
    two = np.concatenate([same * np.cos(turn), same * np.sin(turn)], axis=1)
    return (
        halves(one) + (np.cos(angle).astype(np.float32), np.sin(angle).astype(np.float32)) + halves(two)
    )


def call(kernel, name, *shapes, scratch=()):
    outs = tuple(jax.ShapeDtypeStruct(shape, jnp.float32) for shape in shapes)
    return pl.pallas_call(
        kernel,
        out_shape=outs if len(outs) > 1 else outs[0],
        scratch_shapes=[pltpu.VMEM(shape, jnp.float32) for shape in scratch],
        compiler_params=PARAMS,
        name=name,
    )


def ring(count, step):
    return [(i, (i + step) % count) for i in range(count)]


def shards(populations, fluid_mask):
    relaxed, up, down = call(
        collide_kernel,
        "collide",
        (19, LAYERS, COLUMNS, HEIGHT),
        (Z_ROWS, HEIGHT),
        (Z_ROWS, HEIGHT),
    )(populations, fluid_mask)
    below = lax.ppermute(up, "gz", ring(DEVICES_Z, 1))
    above = lax.ppermute(down, "gz", ring(DEVICES_Z, -1))
    right, left = call(face_kernel, "faces", (X_ROWS, HEIGHT), (X_ROWS, HEIGHT))(
        relaxed, fluid_mask, below, above
    )
    from_left = lax.ppermute(right, "gx", ring(DEVICES_X, 1))
    from_right = lax.ppermute(left, "gx", ring(DEVICES_X, -1))
    sums = call(
        step_kernel,
        "steps",
        (8 * DEVICES_X, HEIGHT),
        scratch=((20, LAYERS, RING, HEIGHT), (19, LAYERS, RING, HEIGHT), (HEIGHT, HEIGHT)),
    )(relaxed, fluid_mask, below, above, from_left, from_right)
    lines = lax.all_to_all(sums, "gx", split_axis=0, concat_axis=0, tiled=True)
    spectrum = call(along_x_kernel, "along_x", (4 * DEVICES_Z, HEIGHT))(lines, *x_table())
    spectrum = lax.all_to_all(spectrum, "gz", split_axis=0, concat_axis=0, tiled=True)
    return call(along_z_kernel, "along_z", (2, 4, 4, NZ))(spectrum, *z_tables())


def solution(mesh):
    placed = (P(None, "gx", "gz", None), P("gx", "gz", None))
    return jax.shard_map(
        shards, mesh=mesh, in_specs=placed, out_specs=P(None, "gx", "gz", None), check_vma=False
    )
```

time: 148 us -> 88.8 us (0.60)
  matrix products: 19.9 us -> 0 us
  starting transfers between devices: 49.7 us -> 30.7 us
  waiting for transfers between devices: 22.4 us -> 4.77 us
  other arithmetic: 11 us -> 0 us
  blocking collectives: 40 us -> 47.9 us
  Pallas kernels: 0 us -> 2.95 us
  local copies, waits for them, and re-layouts: 3.71 us -> 1.88 us
    dot_general x6 -> x0, matrix products: 19.9 us -> none  [the longest x1 4.67 us: shards(): jnp.einsum('ync,nk->yck', real_in, sine, precision=highest)]
    ppermute x8 -> x4, starting transfers between devices: 49.7 us -> 30.7 us  [the longest x1 12 us: shards(): below = lax.ppermute(up, 'gz', ring(DEVICES_Z, 1))]
    ppermute x8 -> x4, waiting for transfers between devices: 22.4 us -> 4.77 us  [the longest x1 3.39 us: shards(): above = lax.ppermute(down, 'gz', ring(DEVICES_Z, -1))]
    all_to_all x2, blocking collectives: 40 us -> 47.9 us  [the longest x1 29.6 us: shards(): lax.all_to_all(spectrum, 'gz', split_axis=0, concat_axis=0, tiled=True)]
    pallas_call x0 -> x5, Pallas kernels: none -> 2.95 us  [the longest x1 1.31 us: shards(): return call(along_z_kernel, 'along_z', (2, 4, 4, NZ))(spectrum, *z_tables())]
    unnamed x34 -> x0, other arithmetic: 1.78 us -> none
    select_n x2 -> x0, other arithmetic: 1.71 us -> none  [collide(): return jnp.where(fluid_cells > 0, relaxed, current)]
    reduce_sum x3 -> x0, other arithmetic: 1.6 us -> none  [the longest x1 1.31 us: collide(): speed_x = jnp.sum(along_x * current, axis=0) / density]
  transfers between devices with their start and end apart: 8 -> 4, of which waited for: 6 -> 2; matrix products, arithmetic and copies ran while one was open for 0% -> 0% of each run, Pallas kernels for 0% -> 0%
where the time goes in v1:
time: 88.8 us; the launch traced here: 88.3 us
  blocking collectives  47.9 us (54%)
  starting transfers between devices  30.7 us (35%)
  waiting for transfers between devices  4.77 us (5%)
  Pallas kernels  2.95 us (3%)
  local copies, waits for them, and re-layouts  1.88 us (2%)
    all_to_all x1, blocking collectives, shards(): lax.all_to_all(spectrum, 'gz', split_axis=0, concat_axis=0, tiled=True)  29.6 us
    all_to_all x1, blocking collectives, shards(): lines = lax.all_to_all(sums, 'gx', split_axis=0, concat_axis=0, tiled=True)  18.3 us
    ppermute x1, starting transfers between devices, shards(): below = lax.ppermute(up, 'gz', ring(DEVICES_Z, 1))  12 us
    ppermute x1, starting transfers between devices, shards(): from_right = lax.ppermute(left, 'gx', ring(DEVICES_X, -1))  8.44 us
    ppermute x1, starting transfers between devices, shards(): above = lax.ppermute(down, 'gz', ring(DEVICES_Z, -1))  5.96 us
    ppermute x1, starting transfers between devices, shards(): from_left = lax.ppermute(right, 'gx', ring(DEVICES_X, 1))  4.3 us
    ppermute x1, waiting for transfers between devices, shards(): above = lax.ppermute(down, 'gz', ring(DEVICES_Z, -1))  3.39 us
    unnamed x20, local copies, waits for them, and re-layouts  1.88 us
  transfers between devices with their start and end apart: 4, of which 2 were waited for; matrix products, arithmetic and copies ran while one was open for 0% of the time, Pallas kernels for 0%

profile of v1, /device:TPU:1, one launch (start us, length us, event | category | flops | bytes accessed | tf_op | source)
XLA Modules:
  0.0 88.3 jit_solution(16123134982057833830)
XLA Ops:
  0.0 0.0 copy-start
  0.0 1.1 %copy-done = f32[19,4,16,128]{3,2,1,0:T(8,128)S(1)} copy-done((f32[19,4,16,128]{3,2,1,0:T(8,128)S(1)}, f32[19,4,16,128]{3,2,1,0:T(8,128)}, u32[]{:S(2)}) %copy-start) | copy-done | bytes 622616
  1.1 0.0 copy-start.1
  1.1 0.8 copy-done.1
  1.8 0.2 collide.1
  2.1 12.0 %collective-permute-start = (f32[104,128]{1,0:T(8,128)S(1)}, f32[104,128]{1,0:T(8,128)S(1)}, u32[]{:S(2)}, u32[]{:S(2)}) collective-permute-start(f32[104,128]{1,0:T(8,128)S(1)} %get-tuple-element.11), channel_id=1, source_target_pairs={{0,1},{1,2},{2,3},{3,4},{4,5},{5,6},{6,7},{7,8},{8,9},{9,10},{10,1... | collective-permute-start | bytes 159752 | tf_op jit(solution)/shard_map/ppermute | solution.py:340
  14.1 6.0 %collective-permute-start.1 = (f32[104,128]{1,0:T(8,128)S(1)}, f32[104,128]{1,0:T(8,128)S(1)}, u32[]{:S(2)}, u32[]{:S(2)}) collective-permute-start(f32[104,128]{1,0:T(8,128)S(1)} %get-tuple-element.12), channel_id=1, source_target_pairs={{0,31},{1,0},{2,1},{3,2},{4,3},{5,4},{6,5},{7,6},{8,7},{9,8},{10,9... | collective-permute-start | bytes 159752 | tf_op jit(solution)/shard_map/ppermute | solution.py:341
  20.1 0.0 collective-permute-done.below
  20.1 3.4 %collective-permute-done.1.above = f32[104,128]{1,0:T(8,128)S(1)} collective-permute-done((f32[104,128]{1,0:T(8,128)S(1)}, f32[104,128]{1,0:T(8,128)S(1)}, u32[]{:S(2)}, u32[]{:S(2)}) %collective-permute-start.1) | collective-permute-done | bytes 53280 | tf_op jit(solution)/shard_map/ppermute | solution.py:341
  23.5 4.3 %collective-permute-start.2 = (f32[144,128]{1,0:T(8,128)S(1)}, f32[144,128]{1,0:T(8,128)S(1)}, u32[]{:S(2)}, u32[]{:S(2)}) collective-permute-start(f32[144,128]{1,0:T(8,128)S(1)} %get-tuple-element.13), channel_id=1, source_target_pairs={{0,32},{32,64},{64,96},{96,128},{128,160},{160,192},{192,224},{224... | collective-permute-start | bytes 221192 | tf_op jit(solution)/shard_map/ppermute | solution.py:345
  27.8 8.4 %collective-permute-start.3 = (f32[144,128]{1,0:T(8,128)S(1)}, f32[144,128]{1,0:T(8,128)S(1)}, u32[]{:S(2)}, u32[]{:S(2)}) collective-permute-start(f32[144,128]{1,0:T(8,128)S(1)} %get-tuple-element.14), channel_id=1, source_target_pairs={{0,992},{32,0},{64,32},{96,64},{128,96},{160,128},{192,160},{224,1... | collective-permute-start | bytes 221192 | tf_op jit(solution)/shard_map/ppermute | solution.py:346
  36.3 0.0 collective-permute-done.2.from_left
  36.3 1.4 %collective-permute-done.3.from_right = f32[144,128]{1,0:T(8,128)S(1)} collective-permute-done((f32[144,128]{1,0:T(8,128)S(1)}, f32[144,128]{1,0:T(8,128)S(1)}, u32[]{:S(2)}, u32[]{:S(2)}) %collective-permute-start.3) | collective-permute-done | bytes 73760 | tf_op jit(solution)/shard_map/ppermute | solution.py:346
  37.7 0.0 copy-start.4
  37.7 0.8 steps.1
  38.5 0.0 copy-start.3
  38.5 18.3 %all_to_all.22 = f32[32,8,128]{2,1,0:T(8,128)S(1)} all-to-all(f32[32,8,128]{2,1,0:T(8,128)S(1)} %bitcast.5), channel_id=1, replica_groups=mesh['gx'=32,'gz'=32] {'gx'}, dimensions={0} | all-to-all | bytes 262144 | tf_op jit(solution)/shard_map/all_to_all | solution.py:353
  56.8 0.0 copy-done.4
  56.8 0.0 copy-done.5
  56.8 0.6 along_x.1
  57.4 0.0 copy-start.6
  57.4 0.0 copy-start.7
  57.4 0.0 copy-start.8
  57.4 0.0 copy-start.9
  57.4 29.6 %all_to_all.23 = f32[32,4,128]{2,1,0:T(4,128)S(1)} all-to-all(f32[32,4,128]{2,1,0:T(4,128)S(1)} %bitcast.7), channel_id=1, replica_groups=mesh['gx'=32,'gz'=32] {'gz'}, dimensions={0} | all-to-all | bytes 131072 | tf_op jit(solution)/shard_map/all_to_all | solution.py:355
  87.0 0.0 copy-done.3
  87.0 0.0 copy-done.2
  87.0 0.0 copy-done.6
  87.0 0.0 copy-done.7
  87.0 0.0 copy-done.8
  87.0 0.0 copy-done.9
  87.0 1.3 %along_z.1 = f32[2,4,4,512]{3,2,1,0:T(4,128)} custom-call(f32[128,128]{1,0:T(8,128)S(1)} %bitcast.6, bf16[64,64]{1,0:T(8,128)(2,1)S(1)} %copy-done.9, bf16[64,64]{1,0:T(8,128)(2,1)S(1)} %copy-done.8, f32[32,256]{1,0:T(8,128)S(1)} %copy-done.7, f32[32,256]{1,0:T(8,128)S(1)} %copy-done.6, bf16[256,512]{1,0:T(8,128)(2,1)S(1)} %copy-done.3, ...), custom_call_target="tpu_custom_call" | custom-call | tf_op jit(solution)/shard_map/along_z/pallas_call | solution.py:356
  (3 shorter events, 0.0 us)
Async XLA Ops:
  0.0 1.1 %copy-start = (f32[19,4,16,128]{3,2,1,0:T(8,128)S(1)}, f32[19,4,16,128]{3,2,1,0:T(8,128)}, u32[]{:S(2)}) copy-start(f32[19,4,16,128]{3,2,1,0:T(8,128)} %pop.1) | copy-start | bytes 1867780
  1.1 0.8 copy-start.1
  2.1 18.0 %collective-permute-start = (f32[104,128]{1,0:T(8,128)S(1)}, f32[104,128]{1,0:T(8,128)S(1)}, u32[]{:S(2)}, u32[]{:S(2)}) collective-permute-start(f32[104,128]{1,0:T(8,128)S(1)} %get-tuple-element.11), channel_id=1, source_target_pairs={{0,1},{1,2},{2,3},{3,4},{4,5},{5,6},{6,7},{7,8},{8,9},{9,10},{10,1... | collective-permute-start | bytes 159752 | tf_op jit(solution)/shard_map/ppermute | solution.py:340
  14.1 9.4 %collective-permute-start.1 = (f32[104,128]{1,0:T(8,128)S(1)}, f32[104,128]{1,0:T(8,128)S(1)}, u32[]{:S(2)}, u32[]{:S(2)}) collective-permute-start(f32[104,128]{1,0:T(8,128)S(1)} %get-tuple-element.12), channel_id=1, source_target_pairs={{0,31},{1,0},{2,1},{3,2},{4,3},{5,4},{6,5},{7,6},{8,7},{9,8},{10,9... | collective-permute-start | bytes 159752 | tf_op jit(solution)/shard_map/ppermute | solution.py:341
  23.5 12.8 %collective-permute-start.2 = (f32[144,128]{1,0:T(8,128)S(1)}, f32[144,128]{1,0:T(8,128)S(1)}, u32[]{:S(2)}, u32[]{:S(2)}) collective-permute-start(f32[144,128]{1,0:T(8,128)S(1)} %get-tuple-element.13), channel_id=1, source_target_pairs={{0,32},{32,64},{64,96},{96,128},{128,160},{160,192},{192,224},{224... | collective-permute-start | bytes 221192 | tf_op jit(solution)/shard_map/ppermute | solution.py:345
  27.8 9.8 %collective-permute-start.3 = (f32[144,128]{1,0:T(8,128)S(1)}, f32[144,128]{1,0:T(8,128)S(1)}, u32[]{:S(2)}, u32[]{:S(2)}) collective-permute-start(f32[144,128]{1,0:T(8,128)S(1)} %get-tuple-element.14), channel_id=1, source_target_pairs={{0,992},{32,0},{64,32},{96,64},{128,96},{160,128},{192,160},{224,1... | collective-permute-start | bytes 221192 | tf_op jit(solution)/shard_map/ppermute | solution.py:346
  37.7 19.2 %copy-start.4 = (bf16[128,256]{1,0:T(8,128)(2,1)S(1)}, bf16[128,256]{1,0:T(8,128)(2,1)}, u32[]{:S(2)}) copy-start(bf16[128,256]{1,0:T(8,128)(2,1)} %constant.17.clone.low) | copy-start | bytes 196612
  37.7 19.2 %copy-start.5 = (bf16[128,256]{1,0:T(8,128)(2,1)S(1)}, bf16[128,256]{1,0:T(8,128)(2,1)}, u32[]{:S(2)}) copy-start(bf16[128,256]{1,0:T(8,128)(2,1)} %constant.16.clone.high) | copy-start | bytes 196612
  38.5 48.5 %copy-start.3 = (bf16[256,512]{1,0:T(8,128)(2,1)S(1)}, bf16[256,512]{1,0:T(8,128)(2,1)}, u32[]{:S(2)}) copy-start(bf16[256,512]{1,0:T(8,128)(2,1)} %constant.22.clone.two_high) | copy-start | bytes 786436
  56.8 30.2 %copy-start.2 = (bf16[256,512]{1,0:T(8,128)(2,1)S(1)}, bf16[256,512]{1,0:T(8,128)(2,1)}, u32[]{:S(2)}) copy-start(bf16[256,512]{1,0:T(8,128)(2,1)} %constant.23.clone.two_low) | copy-start | bytes 786436
  57.4 29.6 %copy-start.6 = (f32[32,256]{1,0:T(8,128)S(1)}, f32[32,256]{1,0:T(8,128)}, u32[]{:S(2)}) copy-start(f32[32,256]{1,0:T(8,128)} %constant.21.clone.twist_sin) | copy-start | bytes 98308
  57.4 29.6 %copy-start.7 = (f32[32,256]{1,0:T(8,128)S(1)}, f32[32,256]{1,0:T(8,128)}, u32[]{:S(2)}) copy-start(f32[32,256]{1,0:T(8,128)} %constant.20.clone.twist_cos) | copy-start | bytes 98308
  57.4 29.6 %copy-start.8 = (bf16[64,64]{1,0:T(8,128)(2,1)S(1)}, bf16[64,64]{1,0:T(8,128)(2,1)}, u32[]{:S(2)}) copy-start(bf16[64,64]{1,0:T(8,128)(2,1)} %constant.19.clone.one_low) | copy-start | bytes 24580
  57.4 29.6 %copy-start.9 = (bf16[64,64]{1,0:T(8,128)(2,1)S(1)}, bf16[64,64]{1,0:T(8,128)(2,1)}, u32[]{:S(2)}) copy-start(bf16[64,64]{1,0:T(8,128)(2,1)} %constant.18.clone.one_high) | copy-start | bytes 24580

commit v2 on v1

--- a/solution.py
+++ b/solution.py
@@ -92,11 +92,23 @@
     return out
 
 
-def collide_kernel(pop, mask, relaxed, up, down):
+def even_index(axis):
+    return lax.axis_index(axis) % 2 == 0
+
+
+def collide_kernel(pop, mask, relaxed, far, near, held, solid, up, down, arrivals):
+    copies = [
+        pltpu.make_async_copy(pop.at[:, x], held.at[:, x], arrivals.at[x]) for x in range(LAYERS)
+    ]
+    copies.append(pltpu.make_async_copy(mask, solid, arrivals.at[LAYERS]))
+    for copy in copies:
+        copy.start()
+    copies[LAYERS].wait()
     for x in range(LAYERS):
-        fluid_here = mask[x].astype(jnp.float32)
-        out = relax([pop[i, x] for i in range(19)], fluid_here > 0)
-        for i in range(19):
+        copies[x].wait()
+        fluid_here = solid[x].astype(jnp.float32)
+        out = relax([held[i, x] for i in range(19)], fluid_here > 0) + [fluid_here]
+        for i in range(20):
             relaxed[i, x] = out[i]
         for send, units, edge, step in (
             (up, Z_UNITS_UP, COLUMNS - 1, -1),
@@ -104,8 +116,10 @@
         ):
             for u, (i, depth) in enumerate(units):
                 z = edge + step * depth
-                value = fluid_here if i == MASK else out[i]
-                send[u * LAYERS + x : u * LAYERS + x + 1, :] = value[z : z + 1, :]
+                send[u * LAYERS + x : u * LAYERS + x + 1, :] = out[i][z : z + 1, :]
+    even = even_index("gz")
+    near[...] = jnp.where(even, up[...], down[...])
+    far[...] = jnp.where(even, down[...], up[...])
 
 
 def ring_tile(i, x, below, above, row):
@@ -118,22 +132,34 @@
     return tile
 
 
-def face_kernel(relaxed, mask, below, above, right, left):
+def face_kernel(relaxed, z_far, z_near, far, near, below, above, right, left):
+    even = even_index("gz")
+    below[...] = jnp.where(even, z_far[...], z_near[...])
+    above[...] = jnp.where(even, z_near[...], z_far[...])
     row = lax.broadcasted_iota(jnp.int32, (8, HEIGHT), 0)
     for send, ids, x in ((right, X_UP, LAYERS - 1), (left, X_DOWN, 0)):
         for v, i in enumerate(ids + (MASK,)):
-            own = mask[x].astype(jnp.float32) if i == MASK else relaxed[i, x]
-            send[v * RING : v * RING + COLUMNS, :] = own
+            send[v * RING : v * RING + COLUMNS, :] = relaxed[i, x]
             send[v * RING + COLUMNS : (v + 1) * RING, :] = ring_tile(i, x, below, above, row)
-
-
-def step_kernel(relaxed, mask, below, above, from_left, from_right, out, first, second, planes):
+    even = even_index("gx")
+    near[...] = jnp.where(even, right[...], left[...])
+    far[...] = jnp.where(even, left[...], right[...])
+
+
+def step_kernel(
+    relaxed, z_far, z_near, x_far, x_near, out, first, second, planes, below, above, from_left, from_right
+):
+    even = even_index("gz")
+    below[...] = jnp.where(even, z_far[...], z_near[...])
+    above[...] = jnp.where(even, z_near[...], z_far[...])
+    even = even_index("gx")
+    from_left[...] = jnp.where(even, x_far[...], x_near[...])
+    from_right[...] = jnp.where(even, x_near[...], x_far[...])
     row = lax.broadcasted_iota(jnp.int32, (8, HEIGHT), 0)
     lane = lax.broadcasted_iota(jnp.int32, (RING, HEIGHT), 1)
     for i in range(20):
         for x in range(LAYERS):
-            own = mask[x].astype(jnp.float32) if i == MASK else relaxed[i, x]
-            first[i, x, 0:COLUMNS] = own
+            first[i, x, 0:COLUMNS] = relaxed[i, x]
             first[i, x, COLUMNS:RING] = ring_tile(i, x, below, above, row)
 
     def moved(value, cy, cz):
@@ -314,42 +340,76 @@
     )
 
 
-def call(kernel, name, *shapes, scratch=()):
+def call(kernel, name, *shapes, scratch=(), in_specs=None):
     outs = tuple(jax.ShapeDtypeStruct(shape, jnp.float32) for shape in shapes)
     return pl.pallas_call(
         kernel,
         out_shape=outs if len(outs) > 1 else outs[0],
-        scratch_shapes=[pltpu.VMEM(shape, jnp.float32) for shape in scratch],
+        **({} if in_specs is None else {"in_specs": in_specs}),
+        scratch_shapes=[
+            pltpu.VMEM(shape, jnp.float32) if isinstance(shape, tuple) else shape
+            for shape in scratch
+        ],
         compiler_params=PARAMS,
         name=name,
     )
 
 
-def ring(count, step):
-    return [(i, (i + step) % count) for i in range(count)]
+def near_pairs(count):
+    return [(i, i ^ 1) for i in range(count)]
+
+
+def far_pairs(count):
+    return [(i, (i + (1 if i % 2 else -1)) % count) for i in range(count)]
+
+
+def swap(near, far, axis, count):
+    near = lax.ppermute(near, axis, near_pairs(count))
+    far = lax.ppermute(far, axis, far_pairs(count))
+    return near, far
 
 
 def shards(populations, fluid_mask):
-    relaxed, up, down = call(
+    block = (LAYERS, COLUMNS, HEIGHT)
+    z_edge = (Z_ROWS, HEIGHT)
+    x_edge = (X_ROWS, HEIGHT)
+    relaxed, far, near = call(
         collide_kernel,
         "collide",
-        (19, LAYERS, COLUMNS, HEIGHT),
-        (Z_ROWS, HEIGHT),
-        (Z_ROWS, HEIGHT),
-    )(populations, fluid_mask)
-    below = lax.ppermute(up, "gz", ring(DEVICES_Z, 1))
-    above = lax.ppermute(down, "gz", ring(DEVICES_Z, -1))
-    right, left = call(face_kernel, "faces", (X_ROWS, HEIGHT), (X_ROWS, HEIGHT))(
-        relaxed, fluid_mask, below, above
-    )
-    from_left = lax.ppermute(right, "gx", ring(DEVICES_X, 1))
-    from_right = lax.ppermute(left, "gx", ring(DEVICES_X, -1))
+        (20,) + block,
+        z_edge,
+        z_edge,
+        in_specs=[pl.BlockSpec(memory_space=pltpu.HBM)] * 2,
+        scratch=(
+            (19,) + block,
+            pltpu.VMEM(block, jnp.int32),
+            z_edge,
+            z_edge,
+            pltpu.SemaphoreType.DMA((LAYERS + 1,)),
+        ),
+    )(
+        pltpu.with_memory_space_constraint(populations, pltpu.HBM),
+        pltpu.with_memory_space_constraint(fluid_mask, pltpu.HBM),
+    )
+    z_near, z_far = swap(near, far, "gz", DEVICES_Z)
+    far, near = call(face_kernel, "faces", x_edge, x_edge, scratch=(z_edge, z_edge, x_edge, x_edge))(
+        relaxed, z_far, z_near
+    )
+    x_near, x_far = swap(near, far, "gx", DEVICES_X)
     sums = call(
         step_kernel,
         "steps",
         (8 * DEVICES_X, HEIGHT),
-        scratch=((20, LAYERS, RING, HEIGHT), (19, LAYERS, RING, HEIGHT), (HEIGHT, HEIGHT)),
-    )(relaxed, fluid_mask, below, above, from_left, from_right)
+        scratch=(
+            (20, LAYERS, RING, HEIGHT),
+            (19, LAYERS, RING, HEIGHT),
+            (HEIGHT, HEIGHT),
+            z_edge,
+            z_edge,
+            x_edge,
+            x_edge,
+        ),
+    )(relaxed, z_far, z_near, x_far, x_near)
     lines = lax.all_to_all(sums, "gx", split_axis=0, concat_axis=0, tiled=True)
     spectrum = call(along_x_kernel, "along_x", (4 * DEVICES_Z, HEIGHT))(lines, *x_table())
     spectrum = lax.all_to_all(spectrum, "gz", split_axis=0, concat_axis=0, tiled=True)

time: 88.8 us -> 83.3 us (0.938)
  blocking collectives: 47.9 us -> 41.6 us
  starting transfers between devices: 30.7 us -> 33 us
  local copies, waits for them, and re-layouts: 1.88 us -> 0.05 us
  Pallas kernels: 2.95 us -> 4.15 us
    all_to_all x1, blocking collectives: 29.6 us -> 25.8 us  [shards(): lax.all_to_all(spectrum, 'gz', split_axis=0, concat_axis=0, tiled=True)]
    all_to_all x1, blocking collectives: 18.3 us -> 15.9 us  [shards(): lines = lax.all_to_all(sums, 'gx', split_axis=0, concat_axis=0, tiled=True)]
    ppermute x4, starting transfers between devices: 30.7 us -> 33 us  [the longest x2 19.9 us: swap(): far = lax.ppermute(far, axis, far_pairs(count))]
    unnamed x20 -> x16, local copies, waits for them, and re-layouts: 1.88 us -> 0.05 us
    pallas_call x2, Pallas kernels: 0.27 us -> 1.43 us  [the longest x1 1.4 us: shards(): call(collide_kernel, 'collide', (20,) + block, z_edge, z_edge, in_specs=[...]
where the time goes in v2:
time: 83.3 us; the launch traced here: 83 us
  blocking collectives  41.6 us (50%)
  starting transfers between devices  33 us (40%)
  Pallas kernels  4.15 us (5%)
  waiting for transfers between devices  4.02 us (5%)
    all_to_all x1, blocking collectives, shards(): lax.all_to_all(spectrum, 'gz', split_axis=0, concat_axis=0, tiled=True)  25.8 us
    ppermute x2, starting transfers between devices, swap(): far = lax.ppermute(far, axis, far_pairs(count))  19.9 us
    all_to_all x1, blocking collectives, shards(): lines = lax.all_to_all(sums, 'gx', split_axis=0, concat_axis=0, tiled=True)  15.9 us
    ppermute x2, starting transfers between devices, swap(): near = lax.ppermute(near, axis, near_pairs(count))  13.1 us
    ppermute x2, waiting for transfers between devices, swap(): near = lax.ppermute(near, axis, near_pairs(count))  4.01 us
  transfers between devices with their start and end apart: 4, of which 2 were waited for; matrix products, arithmetic and copies ran while one was open for 0% of the time, Pallas kernels for 0%

profile of v2, /device:TPU:1, one launch (start us, length us, event | category | flops | bytes accessed | tf_op | source)
XLA Modules:
  0.0 83.0 jit_solution(4532689859352110313)
XLA Ops:
  0.0 1.4 %collide.1 = (f32[20,4,16,128]{3,2,1,0:T(8,128)S(1)}, f32[104,128]{1,0:T(8,128)S(1)}, f32[104,128]{1,0:T(8,128)S(1)}) custom-call(f32[19,4,16,128]{3,2,1,0:T(8,128)} %pop.1, s32[4,16,128]{2,1,0:T(8,128)} %mask.1), custom_call_target="tpu_custom_call" | custom-call | tf_op jit(solution)/shard_map/collide/pallas_call | solution.py:376
  1.4 12.0 %collective-permute-start = (f32[104,128]{1,0:T(8,128)S(1)}, f32[104,128]{1,0:T(8,128)S(1)}, u32[]{:S(2)}, u32[]{:S(2)}) collective-permute-start(f32[104,128]{1,0:T(8,128)S(1)} %get-tuple-element.11), channel_id=1, source_target_pairs={{0,31},{1,2},{2,1},{3,4},{4,3},{5,6},{6,5},{7,8},{8,7},{9,10},{10,... | collective-permute-start | bytes 159752 | tf_op jit(solution)/shard_map/ppermute | solution.py:368
  13.4 11.2 %collective-permute-start.1 = (f32[104,128]{1,0:T(8,128)S(1)}, f32[104,128]{1,0:T(8,128)S(1)}, u32[]{:S(2)}, u32[]{:S(2)}) collective-permute-start(f32[104,128]{1,0:T(8,128)S(1)} %get-tuple-element.12), channel_id=1, source_target_pairs={{0,1},{1,0},{2,3},{3,2},{4,5},{5,4},{6,7},{7,6},{8,9},{9,8},{10,11... | collective-permute-start | bytes 159752 | tf_op jit(solution)/shard_map/ppermute | solution.py:367
  24.7 0.0 collective-permute-done.z_far
  24.7 0.9 %collective-permute-done.1.z_near = f32[104,128]{1,0:T(8,128)S(1)} collective-permute-done((f32[104,128]{1,0:T(8,128)S(1)}, f32[104,128]{1,0:T(8,128)S(1)}, u32[]{:S(2)}, u32[]{:S(2)}) %collective-permute-start.1) | collective-permute-done | bytes 53280 | tf_op jit(solution)/shard_map/ppermute | solution.py:367
  25.6 7.8 %collective-permute-start.2 = (f32[144,128]{1,0:T(8,128)S(1)}, f32[144,128]{1,0:T(8,128)S(1)}, u32[]{:S(2)}, u32[]{:S(2)}) collective-permute-start(f32[144,128]{1,0:T(8,128)S(1)} %get-tuple-element.13), channel_id=1, source_target_pairs={{0,992},{32,64},{64,32},{96,128},{128,96},{160,192},{192,160},{224... | collective-permute-start | bytes 221192 | tf_op jit(solution)/shard_map/ppermute | solution.py:368
  33.4 1.9 %collective-permute-start.3 = (f32[144,128]{1,0:T(8,128)S(1)}, f32[144,128]{1,0:T(8,128)S(1)}, u32[]{:S(2)}, u32[]{:S(2)}) collective-permute-start(f32[144,128]{1,0:T(8,128)S(1)} %get-tuple-element.14), channel_id=1, source_target_pairs={{0,32},{32,0},{64,96},{96,64},{128,160},{160,128},{192,224},{224,1... | collective-permute-start | bytes 221192 | tf_op jit(solution)/shard_map/ppermute | solution.py:367
  35.3 0.0 collective-permute-done.2.x_far
  35.3 3.2 %collective-permute-done.3.x_near = f32[144,128]{1,0:T(8,128)S(1)} collective-permute-done((f32[144,128]{1,0:T(8,128)S(1)}, f32[144,128]{1,0:T(8,128)S(1)}, u32[]{:S(2)}, u32[]{:S(2)}) %collective-permute-start.3) | collective-permute-done | bytes 73760 | tf_op jit(solution)/shard_map/ppermute | solution.py:367
  38.5 0.0 copy-start.2
  38.5 0.0 copy-start.3
  38.5 0.9 %steps.1 = f32[256,128]{1,0:T(8,128)S(1)} custom-call(f32[20,4,16,128]{3,2,1,0:T(8,128)S(1)} %get-tuple-element.10.relaxed, f32[104,128]{1,0:T(8,128)S(1)} %collective-permute-done.z_far, f32[104,128]{1,0:T(8,128)S(1)} %collective-permute-done.1.z_near, f32[144,128]{1,0:T(8,128)S(1)} %collective-permute-done.2.x_far, ...), custom_call_target="tpu_custom_call" | custom-call | tf_op jit(solution)/shard_map/steps/pallas_call | solution.py:399
  39.4 0.0 copy-start.1
  39.4 15.9 %all_to_all.22 = f32[32,8,128]{2,1,0:T(8,128)S(1)} all-to-all(f32[32,8,128]{2,1,0:T(8,128)S(1)} %bitcast.5), channel_id=1, replica_groups=mesh['gx'=32,'gz'=32] {'gx'}, dimensions={0} | all-to-all | bytes 262144 | tf_op jit(solution)/shard_map/all_to_all | solution.py:413
  55.2 0.0 copy-start
  55.2 0.0 copy-done.2
  55.2 0.0 copy-done.3
  55.2 0.6 along_x.1
  55.8 0.0 copy-start.4
  55.8 0.0 copy-start.5
  55.8 0.0 copy-start.6
  55.8 0.0 copy-start.7
  55.8 25.8 %all_to_all.23 = f32[32,4,128]{2,1,0:T(4,128)S(1)} all-to-all(f32[32,4,128]{2,1,0:T(4,128)S(1)} %bitcast.7), channel_id=1, replica_groups=mesh['gx'=32,'gz'=32] {'gz'}, dimensions={0} | all-to-all | bytes 131072 | tf_op jit(solution)/shard_map/all_to_all | solution.py:415
  81.6 0.0 copy-done.1
  81.6 0.0 copy-done
  81.6 0.0 copy-done.4
  81.6 0.0 copy-done.5
  81.6 0.0 copy-done.6
  81.6 0.0 copy-done.7
  81.7 1.3 %along_z.1 = f32[2,4,4,512]{3,2,1,0:T(4,128)} custom-call(f32[128,128]{1,0:T(8,128)S(1)} %bitcast.6, bf16[64,64]{1,0:T(8,128)(2,1)S(1)} %copy-done.7, bf16[64,64]{1,0:T(8,128)(2,1)S(1)} %copy-done.6, f32[32,256]{1,0:T(8,128)S(1)} %copy-done.5, f32[32,256]{1,0:T(8,128)S(1)} %copy-done.4, bf16[256,512]{1,0:T(8,128)(2,1)S(1)} %copy-done.1, ...), custom_call_target="tpu_custom_call" | custom-call | tf_op jit(solution)/shard_map/along_z/pallas_call | solution.py:416
  (1 shorter events, 0.0 us)
Async XLA Ops:
  1.4 23.3 %collective-permute-start = (f32[104,128]{1,0:T(8,128)S(1)}, f32[104,128]{1,0:T(8,128)S(1)}, u32[]{:S(2)}, u32[]{:S(2)}) collective-permute-start(f32[104,128]{1,0:T(8,128)S(1)} %get-tuple-element.11), channel_id=1, source_target_pairs={{0,31},{1,2},{2,1},{3,4},{4,3},{5,6},{6,5},{7,8},{8,7},{9,10},{10,... | collective-permute-start | bytes 159752 | tf_op jit(solution)/shard_map/ppermute | solution.py:368
  13.4 12.1 %collective-permute-start.1 = (f32[104,128]{1,0:T(8,128)S(1)}, f32[104,128]{1,0:T(8,128)S(1)}, u32[]{:S(2)}, u32[]{:S(2)}) collective-permute-start(f32[104,128]{1,0:T(8,128)S(1)} %get-tuple-element.12), channel_id=1, source_target_pairs={{0,1},{1,0},{2,3},{3,2},{4,5},{5,4},{6,7},{7,6},{8,9},{9,8},{10,11... | collective-permute-start | bytes 159752 | tf_op jit(solution)/shard_map/ppermute | solution.py:367
  25.6 9.8 %collective-permute-start.2 = (f32[144,128]{1,0:T(8,128)S(1)}, f32[144,128]{1,0:T(8,128)S(1)}, u32[]{:S(2)}, u32[]{:S(2)}) collective-permute-start(f32[144,128]{1,0:T(8,128)S(1)} %get-tuple-element.13), channel_id=1, source_target_pairs={{0,992},{32,64},{64,32},{96,128},{128,96},{160,192},{192,160},{224... | collective-permute-start | bytes 221192 | tf_op jit(solution)/shard_map/ppermute | solution.py:368
  33.4 5.1 %collective-permute-start.3 = (f32[144,128]{1,0:T(8,128)S(1)}, f32[144,128]{1,0:T(8,128)S(1)}, u32[]{:S(2)}, u32[]{:S(2)}) collective-permute-start(f32[144,128]{1,0:T(8,128)S(1)} %get-tuple-element.14), channel_id=1, source_target_pairs={{0,32},{32,0},{64,96},{96,64},{128,160},{160,128},{192,224},{224,1... | collective-permute-start | bytes 221192 | tf_op jit(solution)/shard_map/ppermute | solution.py:367
  38.5 16.7 %copy-start.2 = (bf16[128,256]{1,0:T(8,128)(2,1)S(1)}, bf16[128,256]{1,0:T(8,128)(2,1)}, u32[]{:S(2)}) copy-start(bf16[128,256]{1,0:T(8,128)(2,1)} %constant.17.clone.low) | copy-start | bytes 196612
  38.5 16.7 %copy-start.3 = (bf16[128,256]{1,0:T(8,128)(2,1)S(1)}, bf16[128,256]{1,0:T(8,128)(2,1)}, u32[]{:S(2)}) copy-start(bf16[128,256]{1,0:T(8,128)(2,1)} %constant.16.clone.high) | copy-start | bytes 196612
  39.4 42.2 %copy-start.1 = (bf16[256,512]{1,0:T(8,128)(2,1)S(1)}, bf16[256,512]{1,0:T(8,128)(2,1)}, u32[]{:S(2)}) copy-start(bf16[256,512]{1,0:T(8,128)(2,1)} %constant.22.clone.two_high) | copy-start | bytes 786436
  55.2 26.4 %copy-start = (bf16[256,512]{1,0:T(8,128)(2,1)S(1)}, bf16[256,512]{1,0:T(8,128)(2,1)}, u32[]{:S(2)}) copy-start(bf16[256,512]{1,0:T(8,128)(2,1)} %constant.23.clone.two_low) | copy-start | bytes 786436
  55.8 25.8 %copy-start.4 = (f32[32,256]{1,0:T(8,128)S(1)}, f32[32,256]{1,0:T(8,128)}, u32[]{:S(2)}) copy-start(f32[32,256]{1,0:T(8,128)} %constant.21.clone.twist_sin) | copy-start | bytes 98308
  55.8 25.8 %copy-start.5 = (f32[32,256]{1,0:T(8,128)S(1)}, f32[32,256]{1,0:T(8,128)}, u32[]{:S(2)}) copy-start(f32[32,256]{1,0:T(8,128)} %constant.20.clone.twist_cos) | copy-start | bytes 98308
  55.8 25.8 %copy-start.6 = (bf16[64,64]{1,0:T(8,128)(2,1)S(1)}, bf16[64,64]{1,0:T(8,128)(2,1)}, u32[]{:S(2)}) copy-start(bf16[64,64]{1,0:T(8,128)(2,1)} %constant.19.clone.one_low) | copy-start | bytes 24580
  55.8 25.8 %copy-start.7 = (bf16[64,64]{1,0:T(8,128)(2,1)S(1)}, bf16[64,64]{1,0:T(8,128)(2,1)}, u32[]{:S(2)}) copy-start(bf16[64,64]{1,0:T(8,128)(2,1)} %constant.18.clone.one_high) | copy-start | bytes 24580

commit v3 on v2

--- a/solution.py
+++ b/solution.py
@@ -45,6 +45,8 @@
 NZ = 512
 MASK = 19
 RING = 24
+FIRST_X = 18
+FIRST_Z = 21
 
 X_UP = tuple(i for i in range(19) if VELOCITIES[i][0] == 1)
 X_DOWN = tuple(i for i in range(19) if VELOCITIES[i][0] == -1)
@@ -235,8 +237,12 @@
     edges = jnp.transpose(planes[...]).reshape(16, 8, HEIGHT)
     for k in range(16):
         a, b = transposed[k], edges[k]
-        out[16 * k : 16 * k + 8, :] = jnp.where(row < 4, a, pltpu.roll(b, 4, 0))
-        out[16 * k + 8 : 16 * k + 16, :] = jnp.where(row < 4, pltpu.roll(a, 4, 0), b)
+        for device, tile in (
+            (2 * k, jnp.where(row < 4, a, pltpu.roll(b, 4, 0))),
+            (2 * k + 1, jnp.where(row < 4, pltpu.roll(a, 4, 0), b)),
+        ):
+            place = 8 * ((device - FIRST_X) % DEVICES_X)
+            out[place : place + 8, :] = tile
 
 
 def split(value):
@@ -318,15 +324,15 @@
 def x_table():
     part, pair, block = np.meshgrid(np.arange(2), np.arange(2), np.arange(32), indexing="ij")
     odd, inner, outer = np.meshgrid(np.arange(2), np.arange(4), np.arange(32), indexing="ij")
-    kx = (4 * block + 2 * pair).reshape(-1, 1) + odd.reshape(1, -1)
-    x = (4 * outer + inner).reshape(1, -1)
+    kx = (4 * ((block + FIRST_Z) % 32) + 2 * pair).reshape(-1, 1) + odd.reshape(1, -1)
+    x = (4 * ((outer + FIRST_X) % 32) + inner).reshape(1, -1)
     angle = 2.0 * np.pi * ((kx * x) % NX) / NX
     scale = 1.0 / (math.sqrt(NX * NZ) * SPEED_UNIT)
     return halves(np.where(part.reshape(-1, 1) == 0, np.cos(angle), -np.sin(angle)) * scale)
 
 
 def z_tables():
-    k, b = np.meshgrid(np.arange(32), np.arange(32), indexing="ij")
+    k, b = np.meshgrid(np.arange(32), (np.arange(32) + FIRST_Z) % 32, indexing="ij")
     angle = 2.0 * np.pi * ((k * b) % 32) / 32
     one = np.block([[np.cos(angle), np.sin(angle)], [-np.sin(angle), np.cos(angle)]])
     angle = 2.0 * np.pi * (np.arange(32)[:, None] * (np.arange(256) % 16)[None, :]) / NZ
@@ -367,6 +373,13 @@
     near = lax.ppermute(near, axis, near_pairs(count))
     far = lax.ppermute(far, axis, far_pairs(count))
     return near, far
+
+
+def exchange(rows, axis, count, first):
+    members = [(first + i) % count for i in range(count)]
+    return lax.all_to_all(
+        rows, axis, split_axis=0, concat_axis=0, tiled=True, axis_index_groups=[members]
+    )
 
 
 def shards(populations, fluid_mask):
@@ -410,9 +423,9 @@
             x_edge,
         ),
     )(relaxed, z_far, z_near, x_far, x_near)
-    lines = lax.all_to_all(sums, "gx", split_axis=0, concat_axis=0, tiled=True)
+    lines = exchange(sums, "gx", DEVICES_X, FIRST_X)
     spectrum = call(along_x_kernel, "along_x", (4 * DEVICES_Z, HEIGHT))(lines, *x_table())
-    spectrum = lax.all_to_all(spectrum, "gz", split_axis=0, concat_axis=0, tiled=True)
+    spectrum = exchange(spectrum, "gz", DEVICES_Z, FIRST_Z)
     return call(along_z_kernel, "along_z", (2, 4, 4, NZ))(spectrum, *z_tables())
 
 

time: 83.3 us -> 74 us (0.89)
  blocking collectives: 41.6 us -> 32.2 us
    all_to_all x2, blocking collectives: 41.6 us -> 32.2 us  [exchange(): lax.all_to_all(rows, axis, split_axis=0, concat_axis=0, tiled=True, axis_...]
where the time goes in v3:
time: 74 us; the launch traced here: 73.6 us
  starting transfers between devices  33 us (45%)
  blocking collectives  32.2 us (44%)
  Pallas kernels  4.15 us (6%)
  waiting for transfers between devices  4.02 us (5%)
    all_to_all x2, blocking collectives, exchange(): lax.all_to_all(rows, axis, split_axis=0, concat_axis=0, tiled=True, axis_...  32.2 us
    ppermute x2, starting transfers between devices, swap(): far = lax.ppermute(far, axis, far_pairs(count))  19.9 us
    ppermute x2, starting transfers between devices, swap(): near = lax.ppermute(near, axis, near_pairs(count))  13.1 us
    ppermute x2, waiting for transfers between devices, swap(): near = lax.ppermute(near, axis, near_pairs(count))  4.01 us
  transfers between devices with their start and end apart: 4, of which 2 were waited for; matrix products, arithmetic and copies ran while one was open for 0% of the time, Pallas kernels for 0%

profile of v3, /device:TPU:1, one launch (start us, length us, event | category | flops | bytes accessed | tf_op | source)
XLA Modules:
  0.0 73.6 jit_solution(12694033152342768413)
XLA Ops:
  0.0 1.4 %collide.1 = (f32[20,4,16,128]{3,2,1,0:T(8,128)S(1)}, f32[104,128]{1,0:T(8,128)S(1)}, f32[104,128]{1,0:T(8,128)S(1)}) custom-call(f32[19,4,16,128]{3,2,1,0:T(8,128)} %pop.1, s32[4,16,128]{2,1,0:T(8,128)} %mask.1), custom_call_target="tpu_custom_call" | custom-call | tf_op jit(solution)/shard_map/collide/pallas_call | solution.py:389
  1.4 12.0 %collective-permute-start = (f32[104,128]{1,0:T(8,128)S(1)}, f32[104,128]{1,0:T(8,128)S(1)}, u32[]{:S(2)}, u32[]{:S(2)}) collective-permute-start(f32[104,128]{1,0:T(8,128)S(1)} %get-tuple-element.11), channel_id=1, source_target_pairs={{0,31},{1,2},{2,1},{3,4},{4,3},{5,6},{6,5},{7,8},{8,7},{9,10},{10,... | collective-permute-start | bytes 159752 | tf_op jit(solution)/shard_map/ppermute | solution.py:374
  13.4 11.2 %collective-permute-start.1 = (f32[104,128]{1,0:T(8,128)S(1)}, f32[104,128]{1,0:T(8,128)S(1)}, u32[]{:S(2)}, u32[]{:S(2)}) collective-permute-start(f32[104,128]{1,0:T(8,128)S(1)} %get-tuple-element.12), channel_id=1, source_target_pairs={{0,1},{1,0},{2,3},{3,2},{4,5},{5,4},{6,7},{7,6},{8,9},{9,8},{10,11... | collective-permute-start | bytes 159752 | tf_op jit(solution)/shard_map/ppermute | solution.py:373
  24.7 0.0 collective-permute-done.z_far
  24.7 0.9 %collective-permute-done.1.z_near = f32[104,128]{1,0:T(8,128)S(1)} collective-permute-done((f32[104,128]{1,0:T(8,128)S(1)}, f32[104,128]{1,0:T(8,128)S(1)}, u32[]{:S(2)}, u32[]{:S(2)}) %collective-permute-start.1) | collective-permute-done | bytes 53280 | tf_op jit(solution)/shard_map/ppermute | solution.py:373
  25.6 7.8 %collective-permute-start.2 = (f32[144,128]{1,0:T(8,128)S(1)}, f32[144,128]{1,0:T(8,128)S(1)}, u32[]{:S(2)}, u32[]{:S(2)}) collective-permute-start(f32[144,128]{1,0:T(8,128)S(1)} %get-tuple-element.13), channel_id=1, source_target_pairs={{0,992},{32,64},{64,32},{96,128},{128,96},{160,192},{192,160},{224... | collective-permute-start | bytes 221192 | tf_op jit(solution)/shard_map/ppermute | solution.py:374
  33.4 1.9 %collective-permute-start.3 = (f32[144,128]{1,0:T(8,128)S(1)}, f32[144,128]{1,0:T(8,128)S(1)}, u32[]{:S(2)}, u32[]{:S(2)}) collective-permute-start(f32[144,128]{1,0:T(8,128)S(1)} %get-tuple-element.14), channel_id=1, source_target_pairs={{0,32},{32,0},{64,96},{96,64},{128,160},{160,128},{192,224},{224,1... | collective-permute-start | bytes 221192 | tf_op jit(solution)/shard_map/ppermute | solution.py:373
  35.3 0.0 collective-permute-done.2.x_far
  35.3 3.2 %collective-permute-done.3.x_near = f32[144,128]{1,0:T(8,128)S(1)} collective-permute-done((f32[144,128]{1,0:T(8,128)S(1)}, f32[144,128]{1,0:T(8,128)S(1)}, u32[]{:S(2)}, u32[]{:S(2)}) %collective-permute-start.3) | collective-permute-done | bytes 73760 | tf_op jit(solution)/shard_map/ppermute | solution.py:373
  38.5 0.0 copy-start.2
  38.5 0.0 copy-start.3
  38.5 0.9 %steps.1 = f32[256,128]{1,0:T(8,128)S(1)} custom-call(f32[20,4,16,128]{3,2,1,0:T(8,128)S(1)} %get-tuple-element.10.relaxed, f32[104,128]{1,0:T(8,128)S(1)} %collective-permute-done.z_far, f32[104,128]{1,0:T(8,128)S(1)} %collective-permute-done.1.z_near, f32[144,128]{1,0:T(8,128)S(1)} %collective-permute-done.2.x_far, ...), custom_call_target="tpu_custom_call" | custom-call | tf_op jit(solution)/shard_map/steps/pallas_call | solution.py:412
  39.4 0.0 copy-start.1
  39.4 12.1 %all_to_all.22 = f32[32,8,128]{2,1,0:T(8,128)S(1)} all-to-all(f32[32,8,128]{2,1,0:T(8,128)S(1)} %bitcast.5), channel_id=1, replica_groups={{576,608,640,672,704,736,768,800,832,864,896,928,960,992,0,32,64,96,128..., dimensions={0} | all-to-all | bytes 262144 | tf_op jit(solution)/shard_map/all_to_all | solution.py:380
  51.5 0.0 copy-start
  51.5 0.0 copy-done.2
  51.5 0.0 copy-done.3
  51.5 0.6 along_x.1
  52.1 0.0 copy-start.4
  52.1 0.0 copy-start.5
  52.1 0.0 copy-start.6
  52.1 0.0 copy-start.7
  52.1 20.1 %all_to_all.23 = f32[32,4,128]{2,1,0:T(4,128)S(1)} all-to-all(f32[32,4,128]{2,1,0:T(4,128)S(1)} %bitcast.7), channel_id=1, replica_groups={{21,22,23,24,25,26,27,28,29,30,31,0,1,2,3,4,5,6,7,8,9,10,11,12,13,14,15..., dimensions={0} | all-to-all | bytes 131072 | tf_op jit(solution)/shard_map/all_to_all | solution.py:380
  72.2 0.0 copy-done.1
  72.2 0.0 copy-done
  72.2 0.0 copy-done.4
  72.2 0.0 copy-done.5
  72.2 0.0 copy-done.6
  72.2 0.0 copy-done.7
  72.3 1.3 %along_z.1 = f32[2,4,4,512]{3,2,1,0:T(4,128)} custom-call(f32[128,128]{1,0:T(8,128)S(1)} %bitcast.6, bf16[64,64]{1,0:T(8,128)(2,1)S(1)} %copy-done.7, bf16[64,64]{1,0:T(8,128)(2,1)S(1)} %copy-done.6, f32[32,256]{1,0:T(8,128)S(1)} %copy-done.5, f32[32,256]{1,0:T(8,128)S(1)} %copy-done.4, bf16[256,512]{1,0:T(8,128)(2,1)S(1)} %copy-done.1, ...), custom_call_target="tpu_custom_call" | custom-call | tf_op jit(solution)/shard_map/along_z/pallas_call | solution.py:429
  (1 shorter events, 0.0 us)
Async XLA Ops:
  1.4 23.3 %collective-permute-start = (f32[104,128]{1,0:T(8,128)S(1)}, f32[104,128]{1,0:T(8,128)S(1)}, u32[]{:S(2)}, u32[]{:S(2)}) collective-permute-start(f32[104,128]{1,0:T(8,128)S(1)} %get-tuple-element.11), channel_id=1, source_target_pairs={{0,31},{1,2},{2,1},{3,4},{4,3},{5,6},{6,5},{7,8},{8,7},{9,10},{10,... | collective-permute-start | bytes 159752 | tf_op jit(solution)/shard_map/ppermute | solution.py:374
  13.4 12.1 %collective-permute-start.1 = (f32[104,128]{1,0:T(8,128)S(1)}, f32[104,128]{1,0:T(8,128)S(1)}, u32[]{:S(2)}, u32[]{:S(2)}) collective-permute-start(f32[104,128]{1,0:T(8,128)S(1)} %get-tuple-element.12), channel_id=1, source_target_pairs={{0,1},{1,0},{2,3},{3,2},{4,5},{5,4},{6,7},{7,6},{8,9},{9,8},{10,11... | collective-permute-start | bytes 159752 | tf_op jit(solution)/shard_map/ppermute | solution.py:373
  25.6 9.8 %collective-permute-start.2 = (f32[144,128]{1,0:T(8,128)S(1)}, f32[144,128]{1,0:T(8,128)S(1)}, u32[]{:S(2)}, u32[]{:S(2)}) collective-permute-start(f32[144,128]{1,0:T(8,128)S(1)} %get-tuple-element.13), channel_id=1, source_target_pairs={{0,992},{32,64},{64,32},{96,128},{128,96},{160,192},{192,160},{224... | collective-permute-start | bytes 221192 | tf_op jit(solution)/shard_map/ppermute | solution.py:374
  33.4 5.1 %collective-permute-start.3 = (f32[144,128]{1,0:T(8,128)S(1)}, f32[144,128]{1,0:T(8,128)S(1)}, u32[]{:S(2)}, u32[]{:S(2)}) collective-permute-start(f32[144,128]{1,0:T(8,128)S(1)} %get-tuple-element.14), channel_id=1, source_target_pairs={{0,32},{32,0},{64,96},{96,64},{128,160},{160,128},{192,224},{224,1... | collective-permute-start | bytes 221192 | tf_op jit(solution)/shard_map/ppermute | solution.py:373
  38.5 13.0 %copy-start.2 = (bf16[128,256]{1,0:T(8,128)(2,1)S(1)}, bf16[128,256]{1,0:T(8,128)(2,1)}, u32[]{:S(2)}) copy-start(bf16[128,256]{1,0:T(8,128)(2,1)} %constant.17.clone.low) | copy-start | bytes 196612
  38.5 13.0 %copy-start.3 = (bf16[128,256]{1,0:T(8,128)(2,1)S(1)}, bf16[128,256]{1,0:T(8,128)(2,1)}, u32[]{:S(2)}) copy-start(bf16[128,256]{1,0:T(8,128)(2,1)} %constant.16.clone.high) | copy-start | bytes 196612
  39.4 32.8 %copy-start.1 = (bf16[256,512]{1,0:T(8,128)(2,1)S(1)}, bf16[256,512]{1,0:T(8,128)(2,1)}, u32[]{:S(2)}) copy-start(bf16[256,512]{1,0:T(8,128)(2,1)} %constant.22.clone.two_high) | copy-start | bytes 786436
  51.5 20.7 %copy-start = (bf16[256,512]{1,0:T(8,128)(2,1)S(1)}, bf16[256,512]{1,0:T(8,128)(2,1)}, u32[]{:S(2)}) copy-start(bf16[256,512]{1,0:T(8,128)(2,1)} %constant.23.clone.two_low) | copy-start | bytes 786436
  52.1 20.2 %copy-start.4 = (f32[32,256]{1,0:T(8,128)S(1)}, f32[32,256]{1,0:T(8,128)}, u32[]{:S(2)}) copy-start(f32[32,256]{1,0:T(8,128)} %constant.21.clone.twist_sin) | copy-start | bytes 98308
  52.1 20.2 %copy-start.5 = (f32[32,256]{1,0:T(8,128)S(1)}, f32[32,256]{1,0:T(8,128)}, u32[]{:S(2)}) copy-start(f32[32,256]{1,0:T(8,128)} %constant.20.clone.twist_cos) | copy-start | bytes 98308
  52.1 20.1 %copy-start.6 = (bf16[64,64]{1,0:T(8,128)(2,1)S(1)}, bf16[64,64]{1,0:T(8,128)(2,1)}, u32[]{:S(2)}) copy-start(bf16[64,64]{1,0:T(8,128)(2,1)} %constant.19.clone.one_low) | copy-start | bytes 24580
  52.1 20.1 %copy-start.7 = (bf16[64,64]{1,0:T(8,128)(2,1)S(1)}, bf16[64,64]{1,0:T(8,128)(2,1)}, u32[]{:S(2)}) copy-start(bf16[64,64]{1,0:T(8,128)(2,1)} %constant.18.clone.one_high) | copy-start | bytes 24580

commit v4 on v2

--- a/solution.py
+++ b/solution.py
@@ -45,6 +45,9 @@
 NZ = 512
 MASK = 19
 RING = 24
+FIRST_X = 18
+SLOT = (0, 2, 3, 1)
+ORDER_Z = tuple((21 + i) % 32 for i in range(32))
 
 X_UP = tuple(i for i in range(19) if VELOCITIES[i][0] == 1)
 X_DOWN = tuple(i for i in range(19) if VELOCITIES[i][0] == -1)
@@ -146,45 +149,57 @@
     far[...] = jnp.where(even, left[...], right[...])
 
 
-def step_kernel(
-    relaxed, z_far, z_near, x_far, x_near, out, first, second, planes, below, above, from_left, from_right
-):
+def moved(value, cy, cz):
+    if cz:
+        value = pltpu.roll(value, cz % RING, 0)
+    if cy:
+        value = pltpu.roll(value, cy % HEIGHT, 1)
+    return value
+
+
+def fluid_moved(value, cy, cz, lane):
+    value = moved(value, cy, cz)
+    if cy:
+        value = jnp.where(lane == (0 if cy == 1 else HEIGHT - 1), 0.0, value)
+    return value > 0
+
+
+def advance(x, source, own, store):
+    lane = lax.broadcasted_iota(jnp.int32, (RING, HEIGHT), 1)
+    fluid = source(MASK, x) > 0
+    arrived = [own(0, x)]
+    for i in range(1, 19):
+        cx, cy, cz = VELOCITIES[i]
+        open_path = fluid_moved(source(MASK, x - cx), cy, cz, lane)
+        value = jnp.where(open_path, moved(source(i, x - cx), cy, cz), own(OPPOSITES[i], x))
+        arrived.append(jnp.where(fluid, value, own(i, x)))
+    for i, value in enumerate(relax(arrived, fluid)):
+        store[i] = value
+
+
+def inner_kernel(relaxed, z_far, z_near, first, second, below, above):
     even = even_index("gz")
     below[...] = jnp.where(even, z_far[...], z_near[...])
     above[...] = jnp.where(even, z_near[...], z_far[...])
-    even = even_index("gx")
-    from_left[...] = jnp.where(even, x_far[...], x_near[...])
-    from_right[...] = jnp.where(even, x_near[...], x_far[...])
     row = lax.broadcasted_iota(jnp.int32, (8, HEIGHT), 0)
-    lane = lax.broadcasted_iota(jnp.int32, (RING, HEIGHT), 1)
     for i in range(20):
         for x in range(LAYERS):
             first[i, x, 0:COLUMNS] = relaxed[i, x]
             first[i, x, COLUMNS:RING] = ring_tile(i, x, below, above, row)
-
-    def moved(value, cy, cz):
-        if cz:
-            value = pltpu.roll(value, cz % RING, 0)
-        if cy:
-            value = pltpu.roll(value, cy % HEIGHT, 1)
-        return value
-
-    def fluid_moved(value, cy, cz):
-        value = moved(value, cy, cz)
-        if cy:
-            value = jnp.where(lane == (0 if cy == 1 else HEIGHT - 1), 0.0, value)
-        return value > 0
+    read = lambda i, x: first[i, x]
+    for x in range(1, LAYERS - 1):
+        advance(x, read, read, second.at[:, x - 1])
+
+
+def outer_kernel(first, inner, x_far, x_near, out, outer, planes, from_left, from_right):
+    even = even_index("gx")
+    from_left[...] = jnp.where(even, x_far[...], x_near[...])
+    from_right[...] = jnp.where(even, x_near[...], x_far[...])
+    lane = lax.broadcasted_iota(jnp.int32, (RING, HEIGHT), 1)
 
     def face(ref, ids, i):
         v = 5 if i == MASK else ids.index(i)
         return ref[v * RING : (v + 1) * RING, :]
-
-    def fluid_at(x):
-        if x < 0:
-            return face(from_left, X_UP, MASK)
-        if x >= LAYERS:
-            return face(from_right, X_DOWN, MASK)
-        return first[MASK, x]
 
     def source(i, x):
         if x < 0:
@@ -193,50 +208,42 @@
             return face(from_right, X_DOWN, i)
         return first[i, x]
 
+    def second(i, x):
+        return outer[i, x // (LAYERS - 1)] if x in (0, LAYERS - 1) else inner[i, x - 1]
+
+    for x in (0, LAYERS - 1):
+        advance(x, source, source, outer.at[:, x // (LAYERS - 1)])
+
+    zero = jnp.zeros((RING, HEIGHT), jnp.float32)
+    place = lambda slot: slice(slot * COLUMNS, (slot + 1) * COLUMNS)
     for x in range(LAYERS):
-        fluid = fluid_at(x) > 0
-        arrived = []
-        for i in range(19):
-            cx, cy, cz = VELOCITIES[i]
-            own = first[i, x]
-            if i == 0:
-                arrived.append(own)
-                continue
-            open_path = fluid_moved(fluid_at(x - cx), cy, cz)
-            value = jnp.where(open_path, moved(source(i, x - cx), cy, cz), first[OPPOSITES[i], x])
-            arrived.append(jnp.where(fluid, value, own))
-        for i, value in enumerate(relax(arrived, fluid)):
-            second[i, x] = value
-
-    zero = jnp.zeros((RING, HEIGHT), jnp.float32)
-    for x in range(LAYERS):
-        fluid = fluid_at(x) > 0
-        groups = {-1: zero, 0: second[0, x], 1: zero}
+        fluid = source(MASK, x) > 0
+        groups = {-1: zero, 0: second(0, x), 1: zero}
         for i in range(1, 19):
             cx, cy, cz = VELOCITIES[i]
-            open_path = fluid_moved(fluid_at(x - cx), cy, cz)
+            open_path = fluid_moved(source(MASK, x - cx), cy, cz, lane)
             inside = 0 <= x - cx < LAYERS
-            value = moved(second[i, x - cx], cy, cz) if inside else zero
-            groups[cx] = groups[cx] + jnp.where(open_path, value, second[OPPOSITES[i], x])
-        number = jnp.where(fluid, groups[1] - groups[-1], 0.0)
-        density = jnp.where(fluid, groups[0] + groups[1] + groups[-1], 1.0)
-        planes[x * COLUMNS : (x + 1) * COLUMNS, :] = number[0:COLUMNS]
-        planes[64 + x * COLUMNS : 64 + (x + 1) * COLUMNS, :] = density[0:COLUMNS]
-    transposed = jnp.transpose(planes[...]).reshape(16, 8, HEIGHT)
-
-    for slot, ids, x, target in ((0, X_DOWN, 0, -1), (1, X_UP, LAYERS - 1, LAYERS)):
+            value = moved(second(i, x - cx), cy, cz) if inside else zero
+            groups[cx] = groups[cx] + jnp.where(open_path, value, second(OPPOSITES[i], x))
+        number = jnp.where(fluid, groups[1] - groups[-1], 0.0)[0:COLUMNS]
+        density = jnp.where(fluid, groups[0] + groups[1] + groups[-1], 1.0)[0:COLUMNS]
+        if x in (0, LAYERS - 1):
+            planes[place(SLOT[x]), :] = number
+            planes[place(SLOT[x] + 4), :] = density
+        else:
+            planes[place(SLOT[x]), :] = number / density
+    for slot, ids, x, target in ((6, X_DOWN, 0, -1), (7, X_UP, LAYERS - 1, LAYERS)):
         total = zero
         for i in ids:
             _, cy, cz = VELOCITIES[i]
-            open_path = fluid_moved(fluid_at(x), cy, cz)
-            total = total + jnp.where(open_path, moved(second[i, x], cy, cz), 0.0)
-        total = jnp.where(fluid_at(target) > 0, total, 0.0)
-        planes[slot * COLUMNS : (slot + 1) * COLUMNS, :] = total[0:COLUMNS]
-    edges = jnp.transpose(planes[...]).reshape(16, 8, HEIGHT)
-    for k in range(16):
-        a, b = transposed[k], edges[k]
-        out[16 * k : 16 * k + 8, :] = jnp.where(row < 4, a, pltpu.roll(b, 4, 0))
-        out[16 * k + 8 : 16 * k + 16, :] = jnp.where(row < 4, pltpu.roll(a, 4, 0), b)
+            open_path = fluid_moved(source(MASK, x), cy, cz, lane)
+            total = total + jnp.where(open_path, moved(second(i, x), cy, cz), 0.0)
+        total = jnp.where(source(MASK, target) > 0, total, 0.0)
+        planes[place(slot), :] = total[0:COLUMNS]
+    turned = jnp.transpose(planes[...])
+    start = 4 * FIRST_X
+    out[0 : HEIGHT - start, :] = turned[start:]
+    out[HEIGHT - start :, :] = turned[:start]
 
 
 def split(value):
@@ -255,26 +262,26 @@
 
 def along_x_kernel(got, high, low, out):
     lane = lax.broadcasted_iota(jnp.int32, (DEVICES_X, HEIGHT), 1)
+    within = lambda slot: (lane >= slot * COLUMNS) & (lane < (slot + 1) * COLUMNS)
     speeds = []
     for y in range(4):
-        own = got[pl.ds(y, DEVICES_X, stride=8), :]
-        edge = got[pl.ds(4 + y, DEVICES_X, stride=8), :]
-        from_left = pltpu.roll(edge, 1, 0)
-        from_right = pltpu.roll(edge, DEVICES_X - 1, 0)
-        total = own + jnp.where(lane < 16, pltpu.roll(from_left, 112, 1), 0.0)
-        total = total + jnp.where((lane >= 64) & (lane < 80), pltpu.roll(from_left, 48, 1), 0.0)
-        total = total - jnp.where((lane >= 48) & (lane < 64), pltpu.roll(from_right, 48, 1), 0.0)
-        total = total + jnp.where(lane >= 112, pltpu.roll(from_right, 112, 1), 0.0)
-        density = jnp.where(lane < 64, pltpu.roll(total, 64, 1), 1.0)
+        own = got[pl.ds(y, DEVICES_X, stride=4), :]
+        from_left = pltpu.roll(own, 1, 0)
+        from_right = pltpu.roll(own, DEVICES_X - 1, 0)
+        total = own + jnp.where(within(0), pltpu.roll(from_left, 16, 1), 0.0)
+        total = total + jnp.where(within(4), pltpu.roll(from_left, 80, 1), 0.0)
+        total = total - jnp.where(within(1), pltpu.roll(from_right, 48, 1), 0.0)
+        total = total + jnp.where(within(5), pltpu.roll(from_right, 112, 1), 0.0)
+        density = jnp.where(lane < 2 * COLUMNS, pltpu.roll(total, 64, 1), 1.0)
         speeds.append(total / density)
     blocks = []
     for shift in (0, 64):
         for x in range(4):
             block = jnp.zeros((DEVICES_X, HEIGHT), jnp.float32)
             for y in range(4):
-                start = shift + 16 * y
-                piece = pltpu.roll(speeds[y], (start - 16 * x) % HEIGHT, 1)
-                block = jnp.where((lane >= start) & (lane < start + 16), piece, block)
+                start = shift + COLUMNS * y
+                piece = pltpu.roll(speeds[y], (start - COLUMNS * SLOT[x]) % HEIGHT, 1)
+                block = jnp.where((lane >= start) & (lane < start + COLUMNS), piece, block)
             blocks.append(block)
     lines = jnp.concatenate(blocks, axis=0)
     result = product((high[...], low[...]), split(lines))
@@ -318,15 +325,15 @@
 def x_table():
     part, pair, block = np.meshgrid(np.arange(2), np.arange(2), np.arange(32), indexing="ij")
     odd, inner, outer = np.meshgrid(np.arange(2), np.arange(4), np.arange(32), indexing="ij")
-    kx = (4 * block + 2 * pair).reshape(-1, 1) + odd.reshape(1, -1)
-    x = (4 * outer + inner).reshape(1, -1)
+    kx = (4 * (np.asarray(ORDER_Z)[block]) + 2 * pair).reshape(-1, 1) + odd.reshape(1, -1)
+    x = (4 * ((outer + FIRST_X) % 32) + inner).reshape(1, -1)
     angle = 2.0 * np.pi * ((kx * x) % NX) / NX
     scale = 1.0 / (math.sqrt(NX * NZ) * SPEED_UNIT)
     return halves(np.where(part.reshape(-1, 1) == 0, np.cos(angle), -np.sin(angle)) * scale)
 
 
 def z_tables():
-    k, b = np.meshgrid(np.arange(32), np.arange(32), indexing="ij")
+    k, b = np.meshgrid(np.arange(32), np.asarray(ORDER_Z), indexing="ij")
     angle = 2.0 * np.pi * ((k * b) % 32) / 32
     one = np.block([[np.cos(angle), np.sin(angle)], [-np.sin(angle), np.cos(angle)]])
     angle = 2.0 * np.pi * (np.arange(32)[:, None] * (np.arange(256) % 16)[None, :]) / NZ
@@ -367,6 +374,12 @@
     near = lax.ppermute(near, axis, near_pairs(count))
     far = lax.ppermute(far, axis, far_pairs(count))
     return near, far
+
+
+def exchange(rows, axis, members):
+    return lax.all_to_all(
+        rows, axis, split_axis=0, concat_axis=0, tiled=True, axis_index_groups=[members]
+    )
 
 
 def shards(populations, fluid_mask):
@@ -396,23 +409,19 @@
         relaxed, z_far, z_near
     )
     x_near, x_far = swap(near, far, "gx", DEVICES_X)
+    ring_block = (LAYERS, RING, HEIGHT)
+    first, inner = call(
+        inner_kernel, "inner", (20,) + ring_block, (19, 2, RING, HEIGHT), scratch=(z_edge, z_edge)
+    )(relaxed, z_far, z_near)
     sums = call(
-        step_kernel,
-        "steps",
-        (8 * DEVICES_X, HEIGHT),
-        scratch=(
-            (20, LAYERS, RING, HEIGHT),
-            (19, LAYERS, RING, HEIGHT),
-            (HEIGHT, HEIGHT),
-            z_edge,
-            z_edge,
-            x_edge,
-            x_edge,
-        ),
-    )(relaxed, z_far, z_near, x_far, x_near)
-    lines = lax.all_to_all(sums, "gx", split_axis=0, concat_axis=0, tiled=True)
+        outer_kernel,
+        "outer",
+        (HEIGHT, HEIGHT),
+        scratch=((19, 2, RING, HEIGHT), (HEIGHT, HEIGHT), x_edge, x_edge),
+    )(first, inner, x_far, x_near)
+    lines = exchange(sums, "gx", [(FIRST_X + i) % DEVICES_X for i in range(DEVICES_X)])
     spectrum = call(along_x_kernel, "along_x", (4 * DEVICES_Z, HEIGHT))(lines, *x_table())
-    spectrum = lax.all_to_all(spectrum, "gz", split_axis=0, concat_axis=0, tiled=True)
+    spectrum = exchange(spectrum, "gz", list(ORDER_Z))
     return call(along_z_kernel, "along_z", (2, 4, 4, NZ))(spectrum, *z_tables())
 
 

time: 83.3 us -> 73.1 us (0.88)
  blocking collectives: 41.6 us -> 31.8 us
    all_to_all x2, blocking collectives: 41.6 us -> 31.8 us  [exchange(): lax.all_to_all(rows, axis, split_axis=0, concat_axis=0, tiled=True, axis_...]
where the time goes in v4:
time: 73.1 us; the launch traced here: 72.8 us
  starting transfers between devices  33 us (45%)
  blocking collectives  31.8 us (44%)
  Pallas kernels  4.16 us (6%)
  waiting for transfers between devices  3.67 us (5%)
    all_to_all x2, blocking collectives, exchange(): lax.all_to_all(rows, axis, split_axis=0, concat_axis=0, tiled=True, axis_...  31.8 us
    ppermute x2, starting transfers between devices, swap(): far = lax.ppermute(far, axis, far_pairs(count))  19.9 us
    ppermute x2, starting transfers between devices, swap(): near = lax.ppermute(near, axis, near_pairs(count))  13.1 us
    ppermute x2, waiting for transfers between devices, swap(): near = lax.ppermute(near, axis, near_pairs(count))  3.67 us
  transfers between devices with their start and end apart: 4, of which 2 were waited for; matrix products, arithmetic and copies ran while one was open for 0% of the time, Pallas kernels for 0%

profile of v4, /device:TPU:1, one launch (start us, length us, event | category | flops | bytes accessed | tf_op | source)
XLA Modules:
  0.0 72.8 jit_solution(11426079842676984289)
XLA Ops:
  0.0 1.4 %collide.1 = (f32[20,4,16,128]{3,2,1,0:T(8,128)S(1)}, f32[104,128]{1,0:T(8,128)S(1)}, f32[104,128]{1,0:T(8,128)S(1)}) custom-call(f32[19,4,16,128]{3,2,1,0:T(8,128)} %pop.1, s32[4,16,128]{2,1,0:T(8,128)} %mask.1), custom_call_target="tpu_custom_call" | custom-call | tf_op jit(solution)/shard_map/collide/pallas_call | solution.py:389
  1.4 12.0 %collective-permute-start = (f32[104,128]{1,0:T(8,128)S(1)}, f32[104,128]{1,0:T(8,128)S(1)}, u32[]{:S(2)}, u32[]{:S(2)}) collective-permute-start(f32[104,128]{1,0:T(8,128)S(1)} %get-tuple-element.13), channel_id=1, source_target_pairs={{0,31},{1,2},{2,1},{3,4},{4,3},{5,6},{6,5},{7,8},{8,7},{9,10},{10,... | collective-permute-start | bytes 159752 | tf_op jit(solution)/shard_map/ppermute | solution.py:375
  13.4 11.2 %collective-permute-start.1 = (f32[104,128]{1,0:T(8,128)S(1)}, f32[104,128]{1,0:T(8,128)S(1)}, u32[]{:S(2)}, u32[]{:S(2)}) collective-permute-start(f32[104,128]{1,0:T(8,128)S(1)} %get-tuple-element.14), channel_id=1, source_target_pairs={{0,1},{1,0},{2,3},{3,2},{4,5},{5,4},{6,7},{7,6},{8,9},{9,8},{10,11... | collective-permute-start | bytes 159752 | tf_op jit(solution)/shard_map/ppermute | solution.py:374
  24.7 0.0 collective-permute-done.z_far
  24.7 0.9 %collective-permute-done.1.z_near = f32[104,128]{1,0:T(8,128)S(1)} collective-permute-done((f32[104,128]{1,0:T(8,128)S(1)}, f32[104,128]{1,0:T(8,128)S(1)}, u32[]{:S(2)}, u32[]{:S(2)}) %collective-permute-start.1) | collective-permute-done | bytes 53280 | tf_op jit(solution)/shard_map/ppermute | solution.py:374
  25.6 7.8 %collective-permute-start.2 = (f32[144,128]{1,0:T(8,128)S(1)}, f32[144,128]{1,0:T(8,128)S(1)}, u32[]{:S(2)}, u32[]{:S(2)}) collective-permute-start(f32[144,128]{1,0:T(8,128)S(1)} %get-tuple-element.17), channel_id=1, source_target_pairs={{0,992},{32,64},{64,32},{96,128},{128,96},{160,192},{192,160},{224... | collective-permute-start | bytes 221192 | tf_op jit(solution)/shard_map/ppermute | solution.py:375
  33.4 1.9 %collective-permute-start.3 = (f32[144,128]{1,0:T(8,128)S(1)}, f32[144,128]{1,0:T(8,128)S(1)}, u32[]{:S(2)}, u32[]{:S(2)}) collective-permute-start(f32[144,128]{1,0:T(8,128)S(1)} %get-tuple-element.18), channel_id=1, source_target_pairs={{0,32},{32,0},{64,96},{96,64},{128,160},{160,128},{192,224},{224,1... | collective-permute-start | bytes 221192 | tf_op jit(solution)/shard_map/ppermute | solution.py:374
  35.3 0.3 inner.1
  35.7 0.0 collective-permute-done.2.x_far
  35.7 2.8 %collective-permute-done.3.x_near = f32[144,128]{1,0:T(8,128)S(1)} collective-permute-done((f32[144,128]{1,0:T(8,128)S(1)}, f32[144,128]{1,0:T(8,128)S(1)}, u32[]{:S(2)}, u32[]{:S(2)}) %collective-permute-start.3) | collective-permute-done | bytes 73760 | tf_op jit(solution)/shard_map/ppermute | solution.py:374
  38.5 0.0 copy-start.2
  38.5 0.0 copy-start.3
  38.5 0.0 copy-start.4
  38.5 0.0 copy-start.5
  38.5 0.0 copy-start.6
  38.5 0.0 copy-start.7
  38.5 0.5 outer.1
  39.1 0.0 copy-start
  39.1 0.0 copy-start.1
  39.1 11.3 %all_to_all.22 = f32[32,4,128]{2,1,0:T(4,128)S(1)} all-to-all(f32[32,4,128]{2,1,0:T(4,128)S(1)} %bitcast.5), channel_id=1, replica_groups={{576,608,640,672,704,736,768,800,832,864,896,928,960,992,0,32,64,96,128..., dimensions={0} | all-to-all | bytes 131072 | tf_op jit(solution)/shard_map/all_to_all | solution.py:380
  50.4 0.0 copy-done.2
  50.4 0.0 copy-done.3
  50.4 0.6 along_x.1
  51.0 20.5 %all_to_all.23 = f32[32,4,128]{2,1,0:T(4,128)S(1)} all-to-all(f32[32,4,128]{2,1,0:T(4,128)S(1)} %bitcast.7), channel_id=1, replica_groups={{21,22,23,24,25,26,27,28,29,30,31,0,1,2,3,4,5,6,7,8,9,10,11,12,13,14,15..., dimensions={0} | all-to-all | bytes 131072 | tf_op jit(solution)/shard_map/all_to_all | solution.py:380
  71.4 0.0 copy-done.4
  71.4 0.0 copy-done.5
  71.4 0.0 copy-done.6
  71.5 0.0 copy-done.7
  71.5 0.0 copy-done
  71.5 0.0 copy-done.1
  71.5 1.3 %along_z.1 = f32[2,4,4,512]{3,2,1,0:T(4,128)} custom-call(f32[128,128]{1,0:T(8,128)S(1)} %bitcast.4, bf16[64,64]{1,0:T(8,128)(2,1)S(1)} %copy-done.7, bf16[64,64]{1,0:T(8,128)(2,1)S(1)} %copy-done.6, f32[32,256]{1,0:T(8,128)S(1)} %copy-done.5, f32[32,256]{1,0:T(8,128)S(1)} %copy-done.4, bf16[256,512]{1,0:T(8,128)(2,1)S(1)} %copy-done.1, ...), custom_call_target="tpu_custom_call" | custom-call | tf_op jit(solution)/shard_map/along_z/pallas_call | solution.py:425
  (1 shorter events, 0.0 us)
Async XLA Ops:
  1.4 23.3 %collective-permute-start = (f32[104,128]{1,0:T(8,128)S(1)}, f32[104,128]{1,0:T(8,128)S(1)}, u32[]{:S(2)}, u32[]{:S(2)}) collective-permute-start(f32[104,128]{1,0:T(8,128)S(1)} %get-tuple-element.13), channel_id=1, source_target_pairs={{0,31},{1,2},{2,1},{3,4},{4,3},{5,6},{6,5},{7,8},{8,7},{9,10},{10,... | collective-permute-start | bytes 159752 | tf_op jit(solution)/shard_map/ppermute | solution.py:375
  13.4 12.1 %collective-permute-start.1 = (f32[104,128]{1,0:T(8,128)S(1)}, f32[104,128]{1,0:T(8,128)S(1)}, u32[]{:S(2)}, u32[]{:S(2)}) collective-permute-start(f32[104,128]{1,0:T(8,128)S(1)} %get-tuple-element.14), channel_id=1, source_target_pairs={{0,1},{1,0},{2,3},{3,2},{4,5},{5,4},{6,7},{7,6},{8,9},{9,8},{10,11... | collective-permute-start | bytes 159752 | tf_op jit(solution)/shard_map/ppermute | solution.py:374
  25.6 10.1 %collective-permute-start.2 = (f32[144,128]{1,0:T(8,128)S(1)}, f32[144,128]{1,0:T(8,128)S(1)}, u32[]{:S(2)}, u32[]{:S(2)}) collective-permute-start(f32[144,128]{1,0:T(8,128)S(1)} %get-tuple-element.17), channel_id=1, source_target_pairs={{0,992},{32,64},{64,32},{96,128},{128,96},{160,192},{192,160},{224... | collective-permute-start | bytes 221192 | tf_op jit(solution)/shard_map/ppermute | solution.py:375
  33.4 5.1 %collective-permute-start.3 = (f32[144,128]{1,0:T(8,128)S(1)}, f32[144,128]{1,0:T(8,128)S(1)}, u32[]{:S(2)}, u32[]{:S(2)}) collective-permute-start(f32[144,128]{1,0:T(8,128)S(1)} %get-tuple-element.18), channel_id=1, source_target_pairs={{0,32},{32,0},{64,96},{96,64},{128,160},{160,128},{192,224},{224,1... | collective-permute-start | bytes 221192 | tf_op jit(solution)/shard_map/ppermute | solution.py:374
  38.5 11.9 %copy-start.2 = (bf16[128,256]{1,0:T(8,128)(2,1)S(1)}, bf16[128,256]{1,0:T(8,128)(2,1)}, u32[]{:S(2)}) copy-start(bf16[128,256]{1,0:T(8,128)(2,1)} %constant.17.clone.low) | copy-start | bytes 196612
  38.5 11.9 %copy-start.3 = (bf16[128,256]{1,0:T(8,128)(2,1)S(1)}, bf16[128,256]{1,0:T(8,128)(2,1)}, u32[]{:S(2)}) copy-start(bf16[128,256]{1,0:T(8,128)(2,1)} %constant.16.clone.high) | copy-start | bytes 196612
  38.5 32.9 %copy-start.4 = (f32[32,256]{1,0:T(8,128)S(1)}, f32[32,256]{1,0:T(8,128)}, u32[]{:S(2)}) copy-start(f32[32,256]{1,0:T(8,128)} %constant.21.clone.twist_sin) | copy-start | bytes 98308
  38.5 32.9 %copy-start.5 = (f32[32,256]{1,0:T(8,128)S(1)}, f32[32,256]{1,0:T(8,128)}, u32[]{:S(2)}) copy-start(f32[32,256]{1,0:T(8,128)} %constant.20.clone.twist_cos) | copy-start | bytes 98308
  38.5 32.9 %copy-start.6 = (bf16[64,64]{1,0:T(8,128)(2,1)S(1)}, bf16[64,64]{1,0:T(8,128)(2,1)}, u32[]{:S(2)}) copy-start(bf16[64,64]{1,0:T(8,128)(2,1)} %constant.19.clone.one_low) | copy-start | bytes 24580
  38.5 32.9 %copy-start.7 = (bf16[64,64]{1,0:T(8,128)(2,1)S(1)}, bf16[64,64]{1,0:T(8,128)(2,1)}, u32[]{:S(2)}) copy-start(bf16[64,64]{1,0:T(8,128)(2,1)} %constant.18.clone.one_high) | copy-start | bytes 24580
  39.1 32.4 %copy-start = (bf16[256,512]{1,0:T(8,128)(2,1)S(1)}, bf16[256,512]{1,0:T(8,128)(2,1)}, u32[]{:S(2)}) copy-start(bf16[256,512]{1,0:T(8,128)(2,1)} %constant.23.clone.two_low) | copy-start | bytes 786436
  39.1 32.4 %copy-start.1 = (bf16[256,512]{1,0:T(8,128)(2,1)S(1)}, bf16[256,512]{1,0:T(8,128)(2,1)}, u32[]{:S(2)}) copy-start(bf16[256,512]{1,0:T(8,128)(2,1)} %constant.22.clone.two_high) | copy-start | bytes 786436

commit v5 on v4

--- a/solution.py
+++ b/solution.py
@@ -104,10 +104,10 @@
         pltpu.make_async_copy(pop.at[:, x], held.at[:, x], arrivals.at[x]) for x in range(LAYERS)
     ]
     copies.append(pltpu.make_async_copy(mask, solid, arrivals.at[LAYERS]))
-    for copy in copies:
+    for copy in copies[::-1]:
         copy.start()
     copies[LAYERS].wait()
-    for x in range(LAYERS):
+    for x in range(LAYERS)[::-1]:
         copies[x].wait()
         fluid_here = solid[x].astype(jnp.float32)
         out = relax([held[i, x] for i in range(19)], fluid_here > 0) + [fluid_here]
@@ -255,12 +255,21 @@
     return jnp.dot(a, b, preferred_element_type=jnp.float32)
 
 
-def product(a, b):
-    (a_high, a_low), (b_high, b_low) = a, b
-    return dot(a_high, b_high) + (dot(a_high, b_low) + dot(a_low, b_high))
-
-
-def along_x_kernel(got, high, low, out):
+def times_split(stacked, value):
+    high, low = split(value)
+    count = stacked.shape[0] // 2
+    both = dot(stacked, high)
+    return both[:count] + (both[count:] + dot(stacked[:count], low))
+
+
+def split_times(value, high, low):
+    stacked = jnp.concatenate(split(value), axis=0)
+    count = value.shape[0]
+    both = dot(stacked, high)
+    return both[:count] + (both[count:] + dot(stacked[:count], low))
+
+
+def along_x_kernel(got, table, out):
     lane = lax.broadcasted_iota(jnp.int32, (DEVICES_X, HEIGHT), 1)
     within = lambda slot: (lane >= slot * COLUMNS) & (lane < (slot + 1) * COLUMNS)
     speeds = []
@@ -275,21 +284,20 @@
         density = jnp.where(lane < 2 * COLUMNS, pltpu.roll(total, 64, 1), 1.0)
         speeds.append(total / density)
     blocks = []
-    for shift in (0, 64):
-        for x in range(4):
-            block = jnp.zeros((DEVICES_X, HEIGHT), jnp.float32)
-            for y in range(4):
-                start = shift + COLUMNS * y
-                piece = pltpu.roll(speeds[y], (start - COLUMNS * SLOT[x]) % HEIGHT, 1)
-                block = jnp.where((lane >= start) & (lane < start + COLUMNS), piece, block)
-            blocks.append(block)
+    for x in range(4):
+        block = jnp.zeros((DEVICES_X, HEIGHT), jnp.float32)
+        for y in range(4):
+            piece = pltpu.roll(speeds[y], (COLUMNS * (y - SLOT[x])) % HEIGHT, 1)
+            block = jnp.where(within(y), piece, block)
+        blocks.append(block)
+    blocks += [pltpu.roll(block, 64, 1) for block in blocks]
     lines = jnp.concatenate(blocks, axis=0)
-    result = product((high[...], low[...]), split(lines))
+    result = times_split(table[...], lines)
     for r in range(4):
         out[pl.ds(r, DEVICES_Z, stride=4), :] = result[32 * r : 32 * r + 32, :]
 
 
-def along_z_kernel(got, one_high, one_low, twist_cos, twist_sin, two_high, two_low, out):
+def along_z_kernel(got, one, twist_cos, twist_sin, two_high, two_low, out):
     rows = [got[pl.ds(r, DEVICES_Z, stride=4), :] for r in range(4)]
     lines = jnp.concatenate(
         [
@@ -298,18 +306,17 @@
         ],
         axis=0,
     )
-    inner = product((one_high[...], one_low[...]), split(lines))
+    inner = times_split(one[...], lines)
     real, imag = inner[0:32], inner[32:64]
     cosine, sine = twist_cos[...], twist_sin[...]
     turned = jnp.concatenate([real * cosine + imag * sine, imag * cosine - real * sine], axis=0)
-    both = product(split(turned), (two_high[...], two_low[...]))
+    both = split_times(turned, two_high[...], two_low[...])
     outer_real = both[0:32, 0:256] + both[32:64, 256:512]
     outer_imag = both[32:64, 0:256] - both[0:32, 256:512]
     for c, value in enumerate((outer_real, outer_imag)):
         columns = jnp.transpose(value)
-        wide = columns.reshape(16, 16, 32)
         for quad in range(4):
-            parts = [wide[:, 4 * quad + k, :] for k in range(4)]
+            parts = [columns[16 * k : 16 * k + 16] for k in range(4 * quad, 4 * quad + 4)]
             tile = jnp.concatenate(parts, axis=1)
             for y in range(4):
                 out[c, y, :, 128 * quad : 128 * quad + 128] = tile[4 * y : 4 * y + 4]
@@ -329,7 +336,8 @@
     x = (4 * ((outer + FIRST_X) % 32) + inner).reshape(1, -1)
     angle = 2.0 * np.pi * ((kx * x) % NX) / NX
     scale = 1.0 / (math.sqrt(NX * NZ) * SPEED_UNIT)
-    return halves(np.where(part.reshape(-1, 1) == 0, np.cos(angle), -np.sin(angle)) * scale)
+    table = halves(np.where(part.reshape(-1, 1) == 0, np.cos(angle), -np.sin(angle)) * scale)
+    return np.concatenate(table, axis=0)
 
 
 def z_tables():
@@ -338,12 +346,15 @@
     one = np.block([[np.cos(angle), np.sin(angle)], [-np.sin(angle), np.cos(angle)]])
     angle = 2.0 * np.pi * (np.arange(32)[:, None] * (np.arange(256) % 16)[None, :]) / NZ
     pair, odd, y, z = (v.reshape(-1, 1) for v in np.unravel_index(np.arange(256), (2, 2, 4, 16)))
-    y_out, kx_out, k_out = (v.reshape(1, -1) for v in np.unravel_index(np.arange(256), (4, 4, 16)))
+    k_out, y_out, kx_out = (v.reshape(1, -1) for v in np.unravel_index(np.arange(256), (16, 4, 4)))
     same = (y == y_out) & (2 * pair + odd == kx_out)
     turn = 2.0 * np.pi * ((z * k_out) % 16) / 16
     two = np.concatenate([same * np.cos(turn), same * np.sin(turn)], axis=1)
     return (
-        halves(one) + (np.cos(angle).astype(np.float32), np.sin(angle).astype(np.float32)) + halves(two)
+        np.concatenate(halves(one), axis=0),
+        np.cos(angle).astype(np.float32),
+        np.sin(angle).astype(np.float32),
+        *halves(two),
     )
 
 
@@ -420,7 +431,7 @@
         scratch=((19, 2, RING, HEIGHT), (HEIGHT, HEIGHT), x_edge, x_edge),
     )(first, inner, x_far, x_near)
     lines = exchange(sums, "gx", [(FIRST_X + i) % DEVICES_X for i in range(DEVICES_X)])
-    spectrum = call(along_x_kernel, "along_x", (4 * DEVICES_Z, HEIGHT))(lines, *x_table())
+    spectrum = call(along_x_kernel, "along_x", (4 * DEVICES_Z, HEIGHT))(lines, x_table())
     spectrum = exchange(spectrum, "gz", list(ORDER_Z))
     return call(along_z_kernel, "along_z", (2, 4, 4, NZ))(spectrum, *z_tables())
 

time: 73.1 us -> 72.9 us (level)
  no operation moved by 1% of the time
where the time goes in v5:
time: 72.9 us; the launch traced here: 72.5 us
  starting transfers between devices  33 us (45%)
  blocking collectives  31.8 us (44%)
  Pallas kernels  3.96 us (5%)
  waiting for transfers between devices  3.67 us (5%)
    all_to_all x2, blocking collectives, exchange(): lax.all_to_all(rows, axis, split_axis=0, concat_axis=0, tiled=True, axis_...  31.8 us
    ppermute x2, starting transfers between devices, swap(): far = lax.ppermute(far, axis, far_pairs(count))  19.9 us
    ppermute x2, starting transfers between devices, swap(): near = lax.ppermute(near, axis, near_pairs(count))  13.1 us
    ppermute x2, waiting for transfers between devices, swap(): near = lax.ppermute(near, axis, near_pairs(count))  3.67 us
  transfers between devices with their start and end apart: 4, of which 2 were waited for; matrix products, arithmetic and copies ran while one was open for 0% of the time, Pallas kernels for 0%

profile of v5, /device:TPU:1, one launch (start us, length us, event | category | flops | bytes accessed | tf_op | source)
XLA Modules:
  0.0 72.5 jit_solution(7456071347654292857)
XLA Ops:
  0.0 1.3 %collide.1 = (f32[20,4,16,128]{3,2,1,0:T(8,128)S(1)}, f32[104,128]{1,0:T(8,128)S(1)}, f32[104,128]{1,0:T(8,128)S(1)}) custom-call(f32[19,4,16,128]{3,2,1,0:T(8,128)} %pop.1, s32[4,16,128]{2,1,0:T(8,128)} %mask.1), custom_call_target="tpu_custom_call" | custom-call | tf_op jit(solution)/shard_map/collide/pallas_call | solution.py:400
  1.3 12.0 %collective-permute-start = (f32[104,128]{1,0:T(8,128)S(1)}, f32[104,128]{1,0:T(8,128)S(1)}, u32[]{:S(2)}, u32[]{:S(2)}) collective-permute-start(f32[104,128]{1,0:T(8,128)S(1)} %get-tuple-element.13), channel_id=1, source_target_pairs={{0,31},{1,2},{2,1},{3,4},{4,3},{5,6},{6,5},{7,8},{8,7},{9,10},{10,... | collective-permute-start | bytes 159752 | tf_op jit(solution)/shard_map/ppermute | solution.py:386
  13.3 11.2 %collective-permute-start.1 = (f32[104,128]{1,0:T(8,128)S(1)}, f32[104,128]{1,0:T(8,128)S(1)}, u32[]{:S(2)}, u32[]{:S(2)}) collective-permute-start(f32[104,128]{1,0:T(8,128)S(1)} %get-tuple-element.14), channel_id=1, source_target_pairs={{0,1},{1,0},{2,3},{3,2},{4,5},{5,4},{6,7},{7,6},{8,9},{9,8},{10,11... | collective-permute-start | bytes 159752 | tf_op jit(solution)/shard_map/ppermute | solution.py:385
  24.5 0.0 collective-permute-done.z_far
  24.6 0.9 %collective-permute-done.1.z_near = f32[104,128]{1,0:T(8,128)S(1)} collective-permute-done((f32[104,128]{1,0:T(8,128)S(1)}, f32[104,128]{1,0:T(8,128)S(1)}, u32[]{:S(2)}, u32[]{:S(2)}) %collective-permute-start.1) | collective-permute-done | bytes 53280 | tf_op jit(solution)/shard_map/ppermute | solution.py:385
  25.4 7.8 %collective-permute-start.2 = (f32[144,128]{1,0:T(8,128)S(1)}, f32[144,128]{1,0:T(8,128)S(1)}, u32[]{:S(2)}, u32[]{:S(2)}) collective-permute-start(f32[144,128]{1,0:T(8,128)S(1)} %get-tuple-element.17), channel_id=1, source_target_pairs={{0,992},{32,64},{64,32},{96,128},{128,96},{160,192},{192,160},{224... | collective-permute-start | bytes 221192 | tf_op jit(solution)/shard_map/ppermute | solution.py:386
  33.3 1.9 %collective-permute-start.3 = (f32[144,128]{1,0:T(8,128)S(1)}, f32[144,128]{1,0:T(8,128)S(1)}, u32[]{:S(2)}, u32[]{:S(2)}) collective-permute-start(f32[144,128]{1,0:T(8,128)S(1)} %get-tuple-element.18), channel_id=1, source_target_pairs={{0,32},{32,0},{64,96},{96,64},{128,160},{160,128},{192,224},{224,1... | collective-permute-start | bytes 221192 | tf_op jit(solution)/shard_map/ppermute | solution.py:385
  35.2 0.3 inner.1
  35.6 0.0 collective-permute-done.2.x_far
  35.6 2.8 %collective-permute-done.3.x_near = f32[144,128]{1,0:T(8,128)S(1)} collective-permute-done((f32[144,128]{1,0:T(8,128)S(1)}, f32[144,128]{1,0:T(8,128)S(1)}, u32[]{:S(2)}, u32[]{:S(2)}) %collective-permute-start.3) | collective-permute-done | bytes 73760 | tf_op jit(solution)/shard_map/ppermute | solution.py:385
  38.4 0.0 copy-start.2
  38.4 0.0 copy-start.3
  38.4 0.0 copy-start.4
  38.4 0.0 copy-start.5
  38.4 0.5 outer.1
  38.9 0.0 copy-start
  38.9 0.0 copy-start.1
  38.9 11.3 %all_to_all.22 = f32[32,4,128]{2,1,0:T(4,128)S(1)} all-to-all(f32[32,4,128]{2,1,0:T(4,128)S(1)} %bitcast.5), channel_id=1, replica_groups={{576,608,640,672,704,736,768,800,832,864,896,928,960,992,0,32,64,96,128..., dimensions={0} | all-to-all | bytes 131072 | tf_op jit(solution)/shard_map/all_to_all | solution.py:391
  50.3 0.0 copy-done.2
  50.3 0.6 along_x.1
  50.9 20.4 %all_to_all.23 = f32[32,4,128]{2,1,0:T(4,128)S(1)} all-to-all(f32[32,4,128]{2,1,0:T(4,128)S(1)} %bitcast.7), channel_id=1, replica_groups={{21,22,23,24,25,26,27,28,29,30,31,0,1,2,3,4,5,6,7,8,9,10,11,12,13,14,15..., dimensions={0} | all-to-all | bytes 131072 | tf_op jit(solution)/shard_map/all_to_all | solution.py:391
  71.3 0.0 copy-done.3
  71.3 0.0 copy-done.4
  71.3 0.0 copy-done.5
  71.3 0.0 copy-done
  71.3 0.0 copy-done.1
  71.3 1.2 %along_z.1 = f32[2,4,4,512]{3,2,1,0:T(4,128)} custom-call(f32[128,128]{1,0:T(8,128)S(1)} %bitcast.4, bf16[128,64]{1,0:T(8,128)(2,1)S(1)} %copy-done.5, f32[32,256]{1,0:T(8,128)S(1)} %copy-done.4, f32[32,256]{1,0:T(8,128)S(1)} %copy-done.3, bf16[256,512]{1,0:T(8,128)(2,1)S(1)} %copy-done.1, bf16[256,512]{1,0:T(8,128)(2,1)S(1)} %copy-done), custom_call_target="tpu_custom_call" | custom-call | tf_op jit(solution)/shard_map/along_z/pallas_call | solution.py:436
  (1 shorter events, 0.0 us)
Async XLA Ops:
  1.3 23.3 %collective-permute-start = (f32[104,128]{1,0:T(8,128)S(1)}, f32[104,128]{1,0:T(8,128)S(1)}, u32[]{:S(2)}, u32[]{:S(2)}) collective-permute-start(f32[104,128]{1,0:T(8,128)S(1)} %get-tuple-element.13), channel_id=1, source_target_pairs={{0,31},{1,2},{2,1},{3,4},{4,3},{5,6},{6,5},{7,8},{8,7},{9,10},{10,... | collective-permute-start | bytes 159752 | tf_op jit(solution)/shard_map/ppermute | solution.py:386
  13.3 12.1 %collective-permute-start.1 = (f32[104,128]{1,0:T(8,128)S(1)}, f32[104,128]{1,0:T(8,128)S(1)}, u32[]{:S(2)}, u32[]{:S(2)}) collective-permute-start(f32[104,128]{1,0:T(8,128)S(1)} %get-tuple-element.14), channel_id=1, source_target_pairs={{0,1},{1,0},{2,3},{3,2},{4,5},{5,4},{6,7},{7,6},{8,9},{9,8},{10,11... | collective-permute-start | bytes 159752 | tf_op jit(solution)/shard_map/ppermute | solution.py:385
  25.4 10.1 %collective-permute-start.2 = (f32[144,128]{1,0:T(8,128)S(1)}, f32[144,128]{1,0:T(8,128)S(1)}, u32[]{:S(2)}, u32[]{:S(2)}) collective-permute-start(f32[144,128]{1,0:T(8,128)S(1)} %get-tuple-element.17), channel_id=1, source_target_pairs={{0,992},{32,64},{64,32},{96,128},{128,96},{160,192},{192,160},{224... | collective-permute-start | bytes 221192 | tf_op jit(solution)/shard_map/ppermute | solution.py:386
  33.3 5.1 %collective-permute-start.3 = (f32[144,128]{1,0:T(8,128)S(1)}, f32[144,128]{1,0:T(8,128)S(1)}, u32[]{:S(2)}, u32[]{:S(2)}) collective-permute-start(f32[144,128]{1,0:T(8,128)S(1)} %get-tuple-element.18), channel_id=1, source_target_pairs={{0,32},{32,0},{64,96},{96,64},{128,160},{160,128},{192,224},{224,1... | collective-permute-start | bytes 221192 | tf_op jit(solution)/shard_map/ppermute | solution.py:385
  38.4 11.9 %copy-start.2 = (bf16[256,256]{1,0:T(8,128)(2,1)S(1)}, bf16[256,256]{1,0:T(8,128)(2,1)}, u32[]{:S(2)}) copy-start(bf16[256,256]{1,0:T(8,128)(2,1)} %constant.12.clone.table) | copy-start | bytes 393220
  38.4 32.9 %copy-start.3 = (f32[32,256]{1,0:T(8,128)S(1)}, f32[32,256]{1,0:T(8,128)}, u32[]{:S(2)}) copy-start(f32[32,256]{1,0:T(8,128)} %constant.15.clone.twist_sin) | copy-start | bytes 98308
  38.4 32.9 %copy-start.4 = (f32[32,256]{1,0:T(8,128)S(1)}, f32[32,256]{1,0:T(8,128)}, u32[]{:S(2)}) copy-start(f32[32,256]{1,0:T(8,128)} %constant.14.clone.twist_cos) | copy-start | bytes 98308
  38.4 32.9 %copy-start.5 = (bf16[128,64]{1,0:T(8,128)(2,1)S(1)}, bf16[128,64]{1,0:T(8,128)(2,1)}, u32[]{:S(2)}) copy-start(bf16[128,64]{1,0:T(8,128)(2,1)} %constant.13.clone.one) | copy-start | bytes 49156
  38.9 32.4 %copy-start = (bf16[256,512]{1,0:T(8,128)(2,1)S(1)}, bf16[256,512]{1,0:T(8,128)(2,1)}, u32[]{:S(2)}) copy-start(bf16[256,512]{1,0:T(8,128)(2,1)} %constant.17.clone.two_low) | copy-start | bytes 786436
  38.9 32.4 %copy-start.1 = (bf16[256,512]{1,0:T(8,128)(2,1)S(1)}, bf16[256,512]{1,0:T(8,128)(2,1)}, u32[]{:S(2)}) copy-start(bf16[256,512]{1,0:T(8,128)(2,1)} %constant.16.clone.two_high) | copy-start | bytes 786436

commit v6 on v5

--- a/solution.py
+++ b/solution.py
@@ -53,9 +53,10 @@
 X_DOWN = tuple(i for i in range(19) if VELOCITIES[i][0] == -1)
 Z_UP = tuple(i for i in range(19) if VELOCITIES[i][2] == 1)
 Z_DOWN = tuple(i for i in range(19) if VELOCITIES[i][2] == -1)
-Z_UNITS_UP = tuple((i, 0) for i in range(20)) + tuple((i, 1) for i in Z_UP + (MASK,))
-Z_UNITS_DOWN = tuple((i, 0) for i in range(20)) + tuple((i, 1) for i in Z_DOWN + (MASK,))
-Z_ROWS = len(Z_UNITS_UP) * LAYERS
+SHIFT = 2
+DEPTH = tuple(4 if i in Z_DOWN + (MASK,) else 3 for i in range(20))
+Z_START = tuple(LAYERS * sum(DEPTH[:i]) for i in range(20))
+Z_ROWS = LAYERS * sum(DEPTH)
 X_ROWS = 6 * RING
 
 PARAMS = pltpu.CompilerParams(vmem_limit_bytes=32 * 1024 * 1024)
@@ -99,7 +100,7 @@
     return lax.axis_index(axis) % 2 == 0
 
 
-def collide_kernel(pop, mask, relaxed, far, near, held, solid, up, down, arrivals):
+def collide_kernel(pop, mask, relaxed, edge, held, solid, arrivals):
     copies = [
         pltpu.make_async_copy(pop.at[:, x], held.at[:, x], arrivals.at[x]) for x in range(LAYERS)
     ]
@@ -113,37 +114,22 @@
         out = relax([held[i, x] for i in range(19)], fluid_here > 0) + [fluid_here]
         for i in range(20):
             relaxed[i, x] = out[i]
-        for send, units, edge, step in (
-            (up, Z_UNITS_UP, COLUMNS - 1, -1),
-            (down, Z_UNITS_DOWN, 0, 1),
-        ):
-            for u, (i, depth) in enumerate(units):
-                z = edge + step * depth
-                send[u * LAYERS + x : u * LAYERS + x + 1, :] = out[i][z : z + 1, :]
-    even = even_index("gz")
-    near[...] = jnp.where(even, up[...], down[...])
-    far[...] = jnp.where(even, down[...], up[...])
-
-
-def ring_tile(i, x, below, above, row):
-    one = lambda ref, u: jnp.broadcast_to(ref[u * LAYERS + x : u * LAYERS + x + 1, :], (8, HEIGHT))
-    tile = jnp.where(row < 4, one(above, i), one(below, i))
-    if (i, 1) in Z_UNITS_DOWN:
-        tile = jnp.where(row == 1, one(above, Z_UNITS_DOWN.index((i, 1))), tile)
-    if (i, 1) in Z_UNITS_UP:
-        tile = jnp.where(row == 6, one(below, Z_UNITS_UP.index((i, 1))), tile)
-    return tile
-
-
-def face_kernel(relaxed, z_far, z_near, far, near, below, above, right, left):
-    even = even_index("gz")
-    below[...] = jnp.where(even, z_far[...], z_near[...])
-    above[...] = jnp.where(even, z_near[...], z_far[...])
-    row = lax.broadcasted_iota(jnp.int32, (8, HEIGHT), 0)
+            start = Z_START[i] + x * DEPTH[i]
+            edge[start : start + DEPTH[i], :] = out[i][0 : DEPTH[i]]
+
+
+def widen(target, i, x, relaxed, beyond):
+    start = Z_START[i] + x * DEPTH[i]
+    target[0:COLUMNS] = relaxed[i, x]
+    target[COLUMNS:RING] = jnp.zeros((RING - COLUMNS, HEIGHT), jnp.float32)
+    target[COLUMNS : COLUMNS + DEPTH[i]] = beyond[start : start + DEPTH[i], :]
+    target[...] = pltpu.roll(target[...], RING - SHIFT, 0)
+
+
+def face_kernel(relaxed, beyond, far, near, right, left):
     for send, ids, x in ((right, X_UP, LAYERS - 1), (left, X_DOWN, 0)):
         for v, i in enumerate(ids + (MASK,)):
-            send[v * RING : v * RING + COLUMNS, :] = relaxed[i, x]
-            send[v * RING + COLUMNS : (v + 1) * RING, :] = ring_tile(i, x, below, above, row)
+            widen(send.at[v * RING : (v + 1) * RING], i, x, relaxed, beyond)
     even = even_index("gx")
     near[...] = jnp.where(even, right[...], left[...])
     far[...] = jnp.where(even, left[...], right[...])
@@ -177,15 +163,10 @@
         store[i] = value
 
 
-def inner_kernel(relaxed, z_far, z_near, first, second, below, above):
-    even = even_index("gz")
-    below[...] = jnp.where(even, z_far[...], z_near[...])
-    above[...] = jnp.where(even, z_near[...], z_far[...])
-    row = lax.broadcasted_iota(jnp.int32, (8, HEIGHT), 0)
+def inner_kernel(relaxed, beyond, first, second):
     for i in range(20):
         for x in range(LAYERS):
-            first[i, x, 0:COLUMNS] = relaxed[i, x]
-            first[i, x, COLUMNS:RING] = ring_tile(i, x, below, above, row)
+            widen(first.at[i, x], i, x, relaxed, beyond)
     read = lambda i, x: first[i, x]
     for x in range(1, LAYERS - 1):
         advance(x, read, read, second.at[:, x - 1])
@@ -344,11 +325,11 @@
     k, b = np.meshgrid(np.arange(32), np.asarray(ORDER_Z), indexing="ij")
     angle = 2.0 * np.pi * ((k * b) % 32) / 32
     one = np.block([[np.cos(angle), np.sin(angle)], [-np.sin(angle), np.cos(angle)]])
-    angle = 2.0 * np.pi * (np.arange(32)[:, None] * (np.arange(256) % 16)[None, :]) / NZ
+    angle = 2.0 * np.pi * (np.arange(32)[:, None] * (np.arange(256) % 16 + SHIFT)[None, :]) / NZ
     pair, odd, y, z = (v.reshape(-1, 1) for v in np.unravel_index(np.arange(256), (2, 2, 4, 16)))
     k_out, y_out, kx_out = (v.reshape(1, -1) for v in np.unravel_index(np.arange(256), (16, 4, 4)))
     same = (y == y_out) & (2 * pair + odd == kx_out)
-    turn = 2.0 * np.pi * ((z * k_out) % 16) / 16
+    turn = 2.0 * np.pi * (((z + SHIFT) * k_out) % 16) / 16
     two = np.concatenate([same * np.cos(turn), same * np.sin(turn)], axis=1)
     return (
         np.concatenate(halves(one), axis=0),
@@ -397,33 +378,28 @@
     block = (LAYERS, COLUMNS, HEIGHT)
     z_edge = (Z_ROWS, HEIGHT)
     x_edge = (X_ROWS, HEIGHT)
-    relaxed, far, near = call(
+    relaxed, edge = call(
         collide_kernel,
         "collide",
         (20,) + block,
-        z_edge,
         z_edge,
         in_specs=[pl.BlockSpec(memory_space=pltpu.HBM)] * 2,
         scratch=(
             (19,) + block,
             pltpu.VMEM(block, jnp.int32),
-            z_edge,
-            z_edge,
             pltpu.SemaphoreType.DMA((LAYERS + 1,)),
         ),
     )(
         pltpu.with_memory_space_constraint(populations, pltpu.HBM),
         pltpu.with_memory_space_constraint(fluid_mask, pltpu.HBM),
     )
-    z_near, z_far = swap(near, far, "gz", DEVICES_Z)
-    far, near = call(face_kernel, "faces", x_edge, x_edge, scratch=(z_edge, z_edge, x_edge, x_edge))(
-        relaxed, z_far, z_near
-    )
+    beyond = lax.ppermute(edge, "gz", [(i, (i - 1) % DEVICES_Z) for i in range(DEVICES_Z)])
+    far, near = call(face_kernel, "faces", x_edge, x_edge, scratch=(x_edge, x_edge))(relaxed, beyond)
     x_near, x_far = swap(near, far, "gx", DEVICES_X)
     ring_block = (LAYERS, RING, HEIGHT)
-    first, inner = call(
-        inner_kernel, "inner", (20,) + ring_block, (19, 2, RING, HEIGHT), scratch=(z_edge, z_edge)
-    )(relaxed, z_far, z_near)
+    first, inner = call(inner_kernel, "inner", (20,) + ring_block, (19, 2, RING, HEIGHT))(
+        relaxed, beyond
+    )
     sums = call(
         outer_kernel,
         "outer",

time: 72.9 us -> 72.4 us (level)
  starting transfers between devices: 33 us -> 26.2 us
  blocking collectives: 31.8 us -> 38.1 us
    ppermute x0 -> x1, starting transfers between devices: none -> 16.1 us  [shards(): lax.ppermute(edge, 'gz', [(i, (i - 1) % DEVICES_Z) for i in range(DEVICES...]
    ppermute x2 -> x1, starting transfers between devices: 19.9 us -> 8.2 us  [swap(): far = lax.ppermute(far, axis, far_pairs(count))]
    ppermute x2 -> x1, starting transfers between devices: 13.1 us -> 1.92 us  [swap(): near = lax.ppermute(near, axis, near_pairs(count))]
    all_to_all x2, blocking collectives: 31.8 us -> 38.1 us  [exchange(): lax.all_to_all(rows, axis, split_axis=0, concat_axis=0, tiled=True, axis_...]
    ppermute x0 -> x1, waiting for transfers between devices: none -> 0.97 us  [shards(): lax.ppermute(edge, 'gz', [(i, (i - 1) % DEVICES_Z) for i in range(DEVICES...]
    ppermute x2 -> x1, waiting for transfers between devices: 3.67 us -> 2.74 us  [swap(): near = lax.ppermute(near, axis, near_pairs(count))]
  transfers between devices with their start and end apart: 4 -> 3, of which waited for: 2 -> 2; matrix products, arithmetic and copies ran while one was open for 0% -> 0% of each run, Pallas kernels for 0% -> 1%
where the time goes in v6:
time: 72.4 us; the launch traced here: 72.2 us
  blocking collectives  38.1 us (53%)
  starting transfers between devices  26.2 us (36%)
  Pallas kernels  4.04 us (6%)
  waiting for transfers between devices  3.71 us (5%)
    all_to_all x2, blocking collectives, exchange(): lax.all_to_all(rows, axis, split_axis=0, concat_axis=0, tiled=True, axis_...  38.1 us
    ppermute x1, starting transfers between devices, shards(): lax.ppermute(edge, 'gz', [(i, (i - 1) % DEVICES_Z) for i in range(DEVICES...  16.1 us
    ppermute x1, starting transfers between devices, swap(): far = lax.ppermute(far, axis, far_pairs(count))  8.2 us
    ppermute x1, waiting for transfers between devices, swap(): near = lax.ppermute(near, axis, near_pairs(count))  2.74 us
    ppermute x1, starting transfers between devices, swap(): near = lax.ppermute(near, axis, near_pairs(count))  1.92 us
  transfers between devices with their start and end apart: 3, of which 2 were waited for; matrix products, arithmetic and copies ran while one was open for 0% of the time, Pallas kernels for 1%

profile of v6, /device:TPU:1, one launch (start us, length us, event | category | flops | bytes accessed | tf_op | source)
XLA Modules:
  0.0 72.2 jit_solution(11461808095629164372)
XLA Ops:
  0.0 1.3 %collide.1 = (f32[20,4,16,128]{3,2,1,0:T(8,128)S(1)}, f32[264,128]{1,0:T(8,128)S(1)}) custom-call(f32[19,4,16,128]{3,2,1,0:T(8,128)} %pop.1, s32[4,16,128]{2,1,0:T(8,128)} %mask.1), custom_call_target="tpu_custom_call" | custom-call | tf_op jit(solution)/shard_map/collide/pallas_call | solution.py:381
  1.3 16.1 %collective-permute-start = (f32[264,128]{1,0:T(8,128)S(1)}, f32[264,128]{1,0:T(8,128)S(1)}, u32[]{:S(2)}, u32[]{:S(2)}) collective-permute-start(f32[264,128]{1,0:T(8,128)S(1)} %get-tuple-element.12), channel_id=1, source_target_pairs={{0,31},{1,0},{2,1},{3,2},{4,3},{5,4},{6,5},{7,6},{8,7},{9,8},{10,9... | collective-permute-start | bytes 405512 | tf_op jit(solution)/shard_map/ppermute | solution.py:396
  17.3 1.0 %collective-permute-done.beyond = f32[264,128]{1,0:T(8,128)S(1)} collective-permute-done((f32[264,128]{1,0:T(8,128)S(1)}, f32[264,128]{1,0:T(8,128)S(1)}, u32[]{:S(2)}, u32[]{:S(2)}) %collective-permute-start) | collective-permute-done | bytes 135200 | tf_op jit(solution)/shard_map/ppermute | solution.py:396
  18.4 8.2 %collective-permute-start.1 = (f32[144,128]{1,0:T(8,128)S(1)}, f32[144,128]{1,0:T(8,128)S(1)}, u32[]{:S(2)}, u32[]{:S(2)}) collective-permute-start(f32[144,128]{1,0:T(8,128)S(1)} %get-tuple-element.15), channel_id=1, source_target_pairs={{0,992},{32,64},{64,32},{96,128},{128,96},{160,192},{192,160},{224... | collective-permute-start | bytes 221192 | tf_op jit(solution)/shard_map/ppermute | solution.py:367
  26.6 1.9 %collective-permute-start.2 = (f32[144,128]{1,0:T(8,128)S(1)}, f32[144,128]{1,0:T(8,128)S(1)}, u32[]{:S(2)}, u32[]{:S(2)}) collective-permute-start(f32[144,128]{1,0:T(8,128)S(1)} %get-tuple-element.16), channel_id=1, source_target_pairs={{0,32},{32,0},{64,96},{96,64},{128,160},{160,128},{192,224},{224,1... | collective-permute-start | bytes 221192 | tf_op jit(solution)/shard_map/ppermute | solution.py:366
  28.5 0.4 inner.1
  28.9 0.0 collective-permute-done.1.x_far
  28.9 2.7 %collective-permute-done.2.x_near = f32[144,128]{1,0:T(8,128)S(1)} collective-permute-done((f32[144,128]{1,0:T(8,128)S(1)}, f32[144,128]{1,0:T(8,128)S(1)}, u32[]{:S(2)}, u32[]{:S(2)}) %collective-permute-start.2) | collective-permute-done | bytes 73760 | tf_op jit(solution)/shard_map/ppermute | solution.py:366
  31.7 0.0 copy-start.2
  31.7 0.0 copy-start.3
  31.7 0.0 copy-start.4
  31.7 0.0 copy-start.5
  31.7 0.5 outer.1
  32.2 0.0 copy-start
  32.2 0.0 copy-start.1
  32.2 11.3 %all_to_all.22 = f32[32,4,128]{2,1,0:T(4,128)S(1)} all-to-all(f32[32,4,128]{2,1,0:T(4,128)S(1)} %bitcast.5), channel_id=1, replica_groups={{576,608,640,672,704,736,768,800,832,864,896,928,960,992,0,32,64,96,128..., dimensions={0} | all-to-all | bytes 131072 | tf_op jit(solution)/shard_map/all_to_all | solution.py:372
  43.6 0.0 copy-done.2
  43.6 0.6 along_x.1
  44.1 26.8 %all_to_all.23 = f32[32,4,128]{2,1,0:T(4,128)S(1)} all-to-all(f32[32,4,128]{2,1,0:T(4,128)S(1)} %bitcast.7), channel_id=1, replica_groups={{21,22,23,24,25,26,27,28,29,30,31,0,1,2,3,4,5,6,7,8,9,10,11,12,13,14,15..., dimensions={0} | all-to-all | bytes 131072 | tf_op jit(solution)/shard_map/all_to_all | solution.py:372
  70.9 0.0 copy-done.3
  70.9 0.0 copy-done.4
  70.9 0.0 copy-done.5
  70.9 0.0 copy-done
  70.9 0.0 copy-done.1
  70.9 1.2 %along_z.1 = f32[2,4,4,512]{3,2,1,0:T(4,128)} custom-call(f32[128,128]{1,0:T(8,128)S(1)} %bitcast.4, bf16[128,64]{1,0:T(8,128)(2,1)S(1)} %copy-done.5, f32[32,256]{1,0:T(8,128)S(1)} %copy-done.4, f32[32,256]{1,0:T(8,128)S(1)} %copy-done.3, bf16[256,512]{1,0:T(8,128)(2,1)S(1)} %copy-done.1, bf16[256,512]{1,0:T(8,128)(2,1)S(1)} %copy-done), custom_call_target="tpu_custom_call" | custom-call | tf_op jit(solution)/shard_map/along_z/pallas_call | solution.py:412
  (1 shorter events, 0.0 us)
Async XLA Ops:
  1.3 17.0 %collective-permute-start = (f32[264,128]{1,0:T(8,128)S(1)}, f32[264,128]{1,0:T(8,128)S(1)}, u32[]{:S(2)}, u32[]{:S(2)}) collective-permute-start(f32[264,128]{1,0:T(8,128)S(1)} %get-tuple-element.12), channel_id=1, source_target_pairs={{0,31},{1,0},{2,1},{3,2},{4,3},{5,4},{6,5},{7,6},{8,7},{9,8},{10,9... | collective-permute-start | bytes 405512 | tf_op jit(solution)/shard_map/ppermute | solution.py:396
  18.4 10.6 %collective-permute-start.1 = (f32[144,128]{1,0:T(8,128)S(1)}, f32[144,128]{1,0:T(8,128)S(1)}, u32[]{:S(2)}, u32[]{:S(2)}) collective-permute-start(f32[144,128]{1,0:T(8,128)S(1)} %get-tuple-element.15), channel_id=1, source_target_pairs={{0,992},{32,64},{64,32},{96,128},{128,96},{160,192},{192,160},{224... | collective-permute-start | bytes 221192 | tf_op jit(solution)/shard_map/ppermute | solution.py:367
  26.6 5.1 %collective-permute-start.2 = (f32[144,128]{1,0:T(8,128)S(1)}, f32[144,128]{1,0:T(8,128)S(1)}, u32[]{:S(2)}, u32[]{:S(2)}) collective-permute-start(f32[144,128]{1,0:T(8,128)S(1)} %get-tuple-element.16), channel_id=1, source_target_pairs={{0,32},{32,0},{64,96},{96,64},{128,160},{160,128},{192,224},{224,1... | collective-permute-start | bytes 221192 | tf_op jit(solution)/shard_map/ppermute | solution.py:366
  31.7 11.9 %copy-start.2 = (bf16[256,256]{1,0:T(8,128)(2,1)S(1)}, bf16[256,256]{1,0:T(8,128)(2,1)}, u32[]{:S(2)}) copy-start(bf16[256,256]{1,0:T(8,128)(2,1)} %constant.12.clone.table) | copy-start | bytes 393220
  31.7 39.2 %copy-start.3 = (f32[32,256]{1,0:T(8,128)S(1)}, f32[32,256]{1,0:T(8,128)}, u32[]{:S(2)}) copy-start(f32[32,256]{1,0:T(8,128)} %constant.15.clone.twist_sin) | copy-start | bytes 98308
  31.7 39.2 %copy-start.4 = (f32[32,256]{1,0:T(8,128)S(1)}, f32[32,256]{1,0:T(8,128)}, u32[]{:S(2)}) copy-start(f32[32,256]{1,0:T(8,128)} %constant.14.clone.twist_cos) | copy-start | bytes 98308
  31.7 39.2 %copy-start.5 = (bf16[128,64]{1,0:T(8,128)(2,1)S(1)}, bf16[128,64]{1,0:T(8,128)(2,1)}, u32[]{:S(2)}) copy-start(bf16[128,64]{1,0:T(8,128)(2,1)} %constant.13.clone.one) | copy-start | bytes 49156
  32.2 38.7 %copy-start = (bf16[256,512]{1,0:T(8,128)(2,1)S(1)}, bf16[256,512]{1,0:T(8,128)(2,1)}, u32[]{:S(2)}) copy-start(bf16[256,512]{1,0:T(8,128)(2,1)} %constant.17.clone.two_low) | copy-start | bytes 786436
  32.2 38.7 %copy-start.1 = (bf16[256,512]{1,0:T(8,128)(2,1)S(1)}, bf16[256,512]{1,0:T(8,128)(2,1)}, u32[]{:S(2)}) copy-start(bf16[256,512]{1,0:T(8,128)(2,1)} %constant.16.clone.two_high) | copy-start | bytes 786436

commit v7 on v6

--- a/solution.py
+++ b/solution.py
@@ -100,11 +100,13 @@
     return lax.axis_index(axis) % 2 == 0
 
 
-def collide_kernel(pop, mask, relaxed, edge, held, solid, arrivals):
+def collide_tile(z, pop, mask, relaxed, edge, held, solid, arrivals):
+    rows = slice(z, z + 8)
     copies = [
-        pltpu.make_async_copy(pop.at[:, x], held.at[:, x], arrivals.at[x]) for x in range(LAYERS)
+        pltpu.make_async_copy(pop.at[:, x, rows], held.at[:, x], arrivals.at[x])
+        for x in range(LAYERS)
     ]
-    copies.append(pltpu.make_async_copy(mask, solid, arrivals.at[LAYERS]))
+    copies.append(pltpu.make_async_copy(mask.at[:, rows], solid, arrivals.at[LAYERS]))
     for copy in copies[::-1]:
         copy.start()
     copies[LAYERS].wait()
@@ -114,22 +116,32 @@
         out = relax([held[i, x] for i in range(19)], fluid_here > 0) + [fluid_here]
         for i in range(20):
             relaxed[i, x] = out[i]
-            start = Z_START[i] + x * DEPTH[i]
-            edge[start : start + DEPTH[i], :] = out[i][0 : DEPTH[i]]
-
-
-def widen(target, i, x, relaxed, beyond):
+            if edge is not None:
+                start = Z_START[i] + x * DEPTH[i]
+                edge[start : start + DEPTH[i], :] = out[i][0 : DEPTH[i]]
+
+
+def low_kernel(pop, mask, relaxed, edge, held, solid, arrivals):
+    collide_tile(0, pop, mask, relaxed, edge, held, solid, arrivals)
+
+
+def high_kernel(pop, mask, relaxed, held, solid, arrivals):
+    collide_tile(8, pop, mask, relaxed, None, held, solid, arrivals)
+
+
+def widen(target, i, x, low, high, beyond):
     start = Z_START[i] + x * DEPTH[i]
-    target[0:COLUMNS] = relaxed[i, x]
+    target[0:8] = low[i, x]
+    target[8:COLUMNS] = high[i, x]
     target[COLUMNS:RING] = jnp.zeros((RING - COLUMNS, HEIGHT), jnp.float32)
     target[COLUMNS : COLUMNS + DEPTH[i]] = beyond[start : start + DEPTH[i], :]
     target[...] = pltpu.roll(target[...], RING - SHIFT, 0)
 
 
-def face_kernel(relaxed, beyond, far, near, right, left):
+def face_kernel(low, high, beyond, far, near, right, left):
     for send, ids, x in ((right, X_UP, LAYERS - 1), (left, X_DOWN, 0)):
         for v, i in enumerate(ids + (MASK,)):
-            widen(send.at[v * RING : (v + 1) * RING], i, x, relaxed, beyond)
+            widen(send.at[v * RING : (v + 1) * RING], i, x, low, high, beyond)
     even = even_index("gx")
     near[...] = jnp.where(even, right[...], left[...])
     far[...] = jnp.where(even, left[...], right[...])
@@ -163,10 +175,10 @@
         store[i] = value
 
 
-def inner_kernel(relaxed, beyond, first, second):
+def inner_kernel(low, high, beyond, first, second):
     for i in range(20):
         for x in range(LAYERS):
-            widen(first.at[i, x], i, x, relaxed, beyond)
+            widen(first.at[i, x], i, x, low, high, beyond)
     read = lambda i, x: first[i, x]
     for x in range(1, LAYERS - 1):
         advance(x, read, read, second.at[:, x - 1])
@@ -375,30 +387,31 @@
 
 
 def shards(populations, fluid_mask):
-    block = (LAYERS, COLUMNS, HEIGHT)
     z_edge = (Z_ROWS, HEIGHT)
     x_edge = (X_ROWS, HEIGHT)
-    relaxed, edge = call(
-        collide_kernel,
-        "collide",
-        (20,) + block,
-        z_edge,
+    tile = (LAYERS, 8, HEIGHT)
+    inputs = (
+        pltpu.with_memory_space_constraint(populations, pltpu.HBM),
+        pltpu.with_memory_space_constraint(fluid_mask, pltpu.HBM),
+    )
+    options = dict(
         in_specs=[pl.BlockSpec(memory_space=pltpu.HBM)] * 2,
         scratch=(
-            (19,) + block,
-            pltpu.VMEM(block, jnp.int32),
+            (19,) + tile,
+            pltpu.VMEM(tile, jnp.int32),
             pltpu.SemaphoreType.DMA((LAYERS + 1,)),
         ),
-    )(
-        pltpu.with_memory_space_constraint(populations, pltpu.HBM),
-        pltpu.with_memory_space_constraint(fluid_mask, pltpu.HBM),
-    )
+    )
+    low, edge = call(low_kernel, "low", (20,) + tile, z_edge, **options)(*inputs)
     beyond = lax.ppermute(edge, "gz", [(i, (i - 1) % DEVICES_Z) for i in range(DEVICES_Z)])
-    far, near = call(face_kernel, "faces", x_edge, x_edge, scratch=(x_edge, x_edge))(relaxed, beyond)
+    high = call(high_kernel, "high", (20,) + tile, **options)(*inputs)
+    far, near = call(face_kernel, "faces", x_edge, x_edge, scratch=(x_edge, x_edge))(
+        low, high, beyond
+    )
     x_near, x_far = swap(near, far, "gx", DEVICES_X)
     ring_block = (LAYERS, RING, HEIGHT)
     first, inner = call(inner_kernel, "inner", (20,) + ring_block, (19, 2, RING, HEIGHT))(
-        relaxed, beyond
+        low, high, beyond
     )
     sums = call(
         outer_kernel,

time: 72.4 us -> 72.4 us (level)
  Pallas kernels: 4.04 us -> 5.05 us
  waiting for transfers between devices: 3.71 us -> 2.74 us
    pallas_call x1 -> x2, Pallas kernels: 1.27 us -> 2.26 us  [the longest x1 1.13 us: shards(): call(low_kernel, 'low', (20,) + tile, z_edge, **options)(*inputs)]
    ppermute x1, waiting for transfers between devices: 0.97 us -> 0.01 us  [shards(): lax.ppermute(edge, 'gz', [(i, (i - 1) % DEVICES_Z) for i in range(DEVICES...]
  transfers between devices with their start and end apart: 3 -> 3, of which waited for: 2 -> 1; matrix products, arithmetic and copies ran while one was open for 0% -> 0% of each run, Pallas kernels for 1% -> 2%
where the time goes in v7:
time: 72.4 us; the launch traced here: 72 us
  blocking collectives  38.1 us (53%)
  starting transfers between devices  26 us (36%)
  Pallas kernels  5.05 us (7%)
  waiting for transfers between devices  2.74 us (4%)
    all_to_all x2, blocking collectives, exchange(): lax.all_to_all(rows, axis, split_axis=0, concat_axis=0, tiled=True, axis_...  38.1 us
    ppermute x1, starting transfers between devices, shards(): lax.ppermute(edge, 'gz', [(i, (i - 1) % DEVICES_Z) for i in range(DEVICES...  16.1 us
    ppermute x1, starting transfers between devices, swap(): far = lax.ppermute(far, axis, far_pairs(count))  8.02 us
    ppermute x1, waiting for transfers between devices, swap(): near = lax.ppermute(near, axis, near_pairs(count))  2.73 us
    ppermute x1, starting transfers between devices, swap(): near = lax.ppermute(near, axis, near_pairs(count))  1.92 us
  transfers between devices with their start and end apart: 3, of which 1 were waited for; matrix products, arithmetic and copies ran while one was open for 0% of the time, Pallas kernels for 2%

profile of v7, /device:TPU:1, one launch (start us, length us, event | category | flops | bytes accessed | tf_op | source)
XLA Modules:
  0.0 72.0 jit_solution(18057910387555131043)
XLA Ops:
  0.0 1.1 %low.1 = (f32[20,4,8,128]{3,2,1,0:T(8,128)S(1)}, f32[264,128]{1,0:T(8,128)S(1)}) custom-call(f32[19,4,16,128]{3,2,1,0:T(8,128)} %pop.3, s32[4,16,128]{2,1,0:T(8,128)} %mask.3), custom_call_target="tpu_custom_call" | custom-call | tf_op jit(solution)/shard_map/low/pallas_call | solution.py:405
  1.1 16.1 %collective-permute-start = (f32[264,128]{1,0:T(8,128)S(1)}, f32[264,128]{1,0:T(8,128)S(1)}, u32[]{:S(2)}, u32[]{:S(2)}) collective-permute-start(f32[264,128]{1,0:T(8,128)S(1)} %get-tuple-element.12), channel_id=1, source_target_pairs={{0,31},{1,0},{2,1},{3,2},{4,3},{5,4},{6,5},{7,6},{8,7},{9,8},{10,9... | collective-permute-start | bytes 405512 | tf_op jit(solution)/shard_map/ppermute | solution.py:406
  17.2 1.1 %high.1 = f32[20,4,8,128]{3,2,1,0:T(8,128)S(1)} custom-call(f32[19,4,16,128]{3,2,1,0:T(8,128)} %pop.3, s32[4,16,128]{2,1,0:T(8,128)} %mask.3), custom_call_target="tpu_custom_call" | custom-call | tf_op jit(solution)/shard_map/high/pallas_call | solution.py:407
  18.3 0.0 collective-permute-done.beyond
  18.4 8.0 %collective-permute-start.1 = (f32[144,128]{1,0:T(8,128)S(1)}, f32[144,128]{1,0:T(8,128)S(1)}, u32[]{:S(2)}, u32[]{:S(2)}) collective-permute-start(f32[144,128]{1,0:T(8,128)S(1)} %get-tuple-element.15), channel_id=1, source_target_pairs={{0,992},{32,64},{64,32},{96,128},{128,96},{160,192},{192,160},{224... | collective-permute-start | bytes 221192 | tf_op jit(solution)/shard_map/ppermute | solution.py:379
  26.4 1.9 %collective-permute-start.2 = (f32[144,128]{1,0:T(8,128)S(1)}, f32[144,128]{1,0:T(8,128)S(1)}, u32[]{:S(2)}, u32[]{:S(2)}) collective-permute-start(f32[144,128]{1,0:T(8,128)S(1)} %get-tuple-element.16), channel_id=1, source_target_pairs={{0,32},{32,0},{64,96},{96,64},{128,160},{160,128},{192,224},{224,1... | collective-permute-start | bytes 221192 | tf_op jit(solution)/shard_map/ppermute | solution.py:378
  28.4 0.4 inner.1
  28.8 0.0 collective-permute-done.1.x_far
  28.8 2.7 %collective-permute-done.2.x_near = f32[144,128]{1,0:T(8,128)S(1)} collective-permute-done((f32[144,128]{1,0:T(8,128)S(1)}, f32[144,128]{1,0:T(8,128)S(1)}, u32[]{:S(2)}, u32[]{:S(2)}) %collective-permute-start.2) | collective-permute-done | bytes 73760 | tf_op jit(solution)/shard_map/ppermute | solution.py:378
  31.5 0.0 copy-start.2
  31.5 0.0 copy-start.3
  31.5 0.0 copy-start.4
  31.5 0.0 copy-start.5
  31.5 0.5 outer.1
  32.1 0.0 copy-start
  32.1 0.0 copy-start.1
  32.1 11.3 %all_to_all.22 = f32[32,4,128]{2,1,0:T(4,128)S(1)} all-to-all(f32[32,4,128]{2,1,0:T(4,128)S(1)} %bitcast.5), channel_id=1, replica_groups={{576,608,640,672,704,736,768,800,832,864,896,928,960,992,0,32,64,96,128..., dimensions={0} | all-to-all | bytes 131072 | tf_op jit(solution)/shard_map/all_to_all | solution.py:384
  43.4 0.0 copy-done.2
  43.4 0.6 along_x.1
  44.0 26.8 %all_to_all.23 = f32[32,4,128]{2,1,0:T(4,128)S(1)} all-to-all(f32[32,4,128]{2,1,0:T(4,128)S(1)} %bitcast.7), channel_id=1, replica_groups={{21,22,23,24,25,26,27,28,29,30,31,0,1,2,3,4,5,6,7,8,9,10,11,12,13,14,15..., dimensions={0} | all-to-all | bytes 131072 | tf_op jit(solution)/shard_map/all_to_all | solution.py:384
  70.8 0.0 copy-done.3
  70.8 0.0 copy-done.4
  70.8 0.0 copy-done.5
  70.8 0.0 copy-done
  70.8 0.0 copy-done.1
  70.8 1.2 %along_z.1 = f32[2,4,4,512]{3,2,1,0:T(4,128)} custom-call(f32[128,128]{1,0:T(8,128)S(1)} %bitcast.4, bf16[128,64]{1,0:T(8,128)(2,1)S(1)} %copy-done.5, f32[32,256]{1,0:T(8,128)S(1)} %copy-done.4, f32[32,256]{1,0:T(8,128)S(1)} %copy-done.3, bf16[256,512]{1,0:T(8,128)(2,1)S(1)} %copy-done.1, bf16[256,512]{1,0:T(8,128)(2,1)S(1)} %copy-done), custom_call_target="tpu_custom_call" | custom-call | tf_op jit(solution)/shard_map/along_z/pallas_call | solution.py:425
  (1 shorter events, 0.0 us)
Async XLA Ops:
  1.1 17.2 %collective-permute-start = (f32[264,128]{1,0:T(8,128)S(1)}, f32[264,128]{1,0:T(8,128)S(1)}, u32[]{:S(2)}, u32[]{:S(2)}) collective-permute-start(f32[264,128]{1,0:T(8,128)S(1)} %get-tuple-element.12), channel_id=1, source_target_pairs={{0,31},{1,0},{2,1},{3,2},{4,3},{5,4},{6,5},{7,6},{8,7},{9,8},{10,9... | collective-permute-start | bytes 405512 | tf_op jit(solution)/shard_map/ppermute | solution.py:406
  18.4 10.4 %collective-permute-start.1 = (f32[144,128]{1,0:T(8,128)S(1)}, f32[144,128]{1,0:T(8,128)S(1)}, u32[]{:S(2)}, u32[]{:S(2)}) collective-permute-start(f32[144,128]{1,0:T(8,128)S(1)} %get-tuple-element.15), channel_id=1, source_target_pairs={{0,992},{32,64},{64,32},{96,128},{128,96},{160,192},{192,160},{224... | collective-permute-start | bytes 221192 | tf_op jit(solution)/shard_map/ppermute | solution.py:379
  26.4 5.1 %collective-permute-start.2 = (f32[144,128]{1,0:T(8,128)S(1)}, f32[144,128]{1,0:T(8,128)S(1)}, u32[]{:S(2)}, u32[]{:S(2)}) collective-permute-start(f32[144,128]{1,0:T(8,128)S(1)} %get-tuple-element.16), channel_id=1, source_target_pairs={{0,32},{32,0},{64,96},{96,64},{128,160},{160,128},{192,224},{224,1... | collective-permute-start | bytes 221192 | tf_op jit(solution)/shard_map/ppermute | solution.py:378
  31.5 11.9 %copy-start.2 = (bf16[256,256]{1,0:T(8,128)(2,1)S(1)}, bf16[256,256]{1,0:T(8,128)(2,1)}, u32[]{:S(2)}) copy-start(bf16[256,256]{1,0:T(8,128)(2,1)} %constant.12.clone.table) | copy-start | bytes 393220
  31.5 39.2 %copy-start.3 = (f32[32,256]{1,0:T(8,128)S(1)}, f32[32,256]{1,0:T(8,128)}, u32[]{:S(2)}) copy-start(f32[32,256]{1,0:T(8,128)} %constant.15.clone.twist_sin) | copy-start | bytes 98308
  31.5 39.2 %copy-start.4 = (f32[32,256]{1,0:T(8,128)S(1)}, f32[32,256]{1,0:T(8,128)}, u32[]{:S(2)}) copy-start(f32[32,256]{1,0:T(8,128)} %constant.14.clone.twist_cos) | copy-start | bytes 98308
  31.5 39.2 %copy-start.5 = (bf16[128,64]{1,0:T(8,128)(2,1)S(1)}, bf16[128,64]{1,0:T(8,128)(2,1)}, u32[]{:S(2)}) copy-start(bf16[128,64]{1,0:T(8,128)(2,1)} %constant.13.clone.one) | copy-start | bytes 49156
  32.1 38.7 %copy-start = (bf16[256,512]{1,0:T(8,128)(2,1)S(1)}, bf16[256,512]{1,0:T(8,128)(2,1)}, u32[]{:S(2)}) copy-start(bf16[256,512]{1,0:T(8,128)(2,1)} %constant.17.clone.two_low) | copy-start | bytes 786436
  32.1 38.7 %copy-start.1 = (bf16[256,512]{1,0:T(8,128)(2,1)S(1)}, bf16[256,512]{1,0:T(8,128)(2,1)}, u32[]{:S(2)}) copy-start(bf16[256,512]{1,0:T(8,128)(2,1)} %constant.16.clone.two_high) | copy-start | bytes 786436
